TPU v7x, 32 devices: a whole 2x2x4 slice. The times are simulated.
32 devices in a mesh: dp: 4 (over x, core), fsdp: 8 (over z, y).
Axes of the slice: x: 2, y: 2, z: 4, core: 2. Of those that a mesh axis runs over, the one named last changes fastest.
Arguments:
- hidden: bfloat16 [32, 128, 768], P(('dp', 'fsdp')), may hold values from -6 to 6
- sections: int32 [32], P(('dp', 'fsdp')), may hold values from 0 to 3
- lengths: int32 [32], P(('dp', 'fsdp')), may hold values from 32 to 128, as said below
- token_mask: int32 [32, 128], P(('dp', 'fsdp')), may hold values 0 or 1
- cotangent: bfloat16 [32, 128, 768], P(('dp', 'fsdp')), may hold values from -6 to 6
- ln1_gain: bfloat16 [768], P(('dp', 'fsdp')), may hold values from 0.5 to 1.5
- ln1_bias: bfloat16 [768], P(('dp', 'fsdp')), may hold values from -1.5 to 1.5
- qkv_weight: bfloat16 [768, 2304], P(('dp', 'fsdp')), may hold values from -0.21875 to 0.21875
- qv_bias: bfloat16 [1536], P(('dp', 'fsdp')), may hold values from -1.5 to 1.5
- out_weight: bfloat16 [768, 768], P(('dp', 'fsdp')), may hold values from -0.875 to 0.875
- out_bias: bfloat16 [768], P(('dp', 'fsdp')), may hold values from -1.5 to 1.5
- ln2_gain: bfloat16 [768], P(('dp', 'fsdp')), may hold values from 0.5 to 1.5
- ln2_bias: bfloat16 [768], P(('dp', 'fsdp')), may hold values from -1.5 to 1.5
- fc_weight: bfloat16 [768, 3072], P(('dp', 'fsdp')), may hold values from -0.21875 to 0.21875
- fc_bias: bfloat16 [3072], P(('dp', 'fsdp')), may hold values from -1.5 to 1.5
- proj_weight: bfloat16 [3072, 768], P(('dp', 'fsdp')), may hold values from -0.109375 to 0.109375
- proj_bias: bfloat16 [768], P(('dp', 'fsdp')), may hold values from -1.5 to 1.5
Outputs:
- hidden_out: bfloat16 [32, 128, 768], P(('dp', 'fsdp'))
- grad_hidden: float32 [32, 128, 768], P(('dp', 'fsdp'))
- grad_ln1_gain: float32 [768], P(('dp', 'fsdp'))
- grad_ln1_bias: float32 [768], P(('dp', 'fsdp'))
- grad_qkv_weight: float32 [768, 2304], P(('dp', 'fsdp'))
- grad_qv_bias: float32 [1536], P(('dp', 'fsdp'))
- grad_out_weight: float32 [768, 768], P(('dp', 'fsdp'))
- grad_out_bias: float32 [768], P(('dp', 'fsdp'))
- grad_ln2_gain: float32 [768], P(('dp', 'fsdp'))
- grad_ln2_bias: float32 [768], P(('dp', 'fsdp'))
- grad_fc_weight: float32 [768, 3072], P(('dp', 'fsdp'))
- grad_fc_bias: float32 [3072], P(('dp', 'fsdp'))
- grad_proj_weight: float32 [3072, 768], P(('dp', 'fsdp'))
- grad_proj_bias: float32 [768], P(('dp', 'fsdp'))
Inputs may be any that keep to these rules, and one draw needn't show every extreme that they name: `lengths`: some sequence has exactly 128 valid tokens and some has exactly 32.
All inputs are finite; a program needn't handle non-finite values. No bound on the sum of `token_mask` on one device may be relied on, other than what follows from the above.
Results may differ from a plain program's by a relative error of at most 0.013.
Values may be sent and summed in bfloat16 or wider, within the bound.
A program may use at most 192 MiB of HBM per device.

v0:
```python
import functools
import itertools

import jax
import jax.numpy as jnp
from jax import lax
from jax.experimental import pallas as pl
from jax.experimental.pallas import tpu as pltpu
from jax.sharding import PartitionSpec as P
MESH = pl.DeviceIdType.MESH

TREES = ("zyx", "zxy", "xyz")


def offsets(length):
    return [0, "o"] if length == 2 else list(range(-(length - 1), length))


class Place:
    def __init__(self, sizes):
        self.sizes = sizes
        dp, fs = lax.axis_index("dp"), lax.axis_index("fsdp")
        self.core = lax.rem(dp, 2)
        self.pos = {"x": dp // 2, "z": fs // sizes["y"], "y": lax.rem(fs, sizes["y"])}

    def device(self, pos, core):
        return (pos["x"] * 2 + core, pos["z"] * self.sizes["y"] + pos["y"])

    def index(self, pos, core):
        dp, fs = self.device(pos, core)
        return dp * (self.sizes["z"] * self.sizes["y"]) + fs

    def chip(self, pos):
        return (pos["x"] * self.sizes["z"] + pos["z"]) * self.sizes["y"] + pos["y"]

    def neighbours(self):
        out = [(None, self.device(self.pos, 1 - self.core))]
        for d, length in self.sizes.items():
            if length == 2:
                out.append((None, self.device({**self.pos, d: 1 - self.pos[d]}, self.core)))
            elif length > 2:
                for s in (1, -1):
                    q = self.pos[d] + s
                    out.append(((q >= 0) & (q < length), self.device({**self.pos, d: q}, self.core)))
        return out


def when(conds, fn):
    conds = [c for c in conds if c is not None]
    if not conds:
        fn()
    else:
        pl.when(functools.reduce(jnp.logical_and, conds))(lambda: (fn(), None)[1])


def entry_barrier(place):
    barrier = pltpu.get_barrier_semaphore()
    total = 0
    for cond, dev in place.neighbours():
        when([cond], lambda dev=dev: pl.semaphore_signal(barrier, inc=1, device_id=dev, device_id_type=MESH))
        total = total + (1 if cond is None else cond.astype(jnp.int32))
    pl.semaphore_wait(barrier, total)


def gather_kernel(sizes, pieces, order, n_in, *refs):
    ins, outs = refs[:n_in], refs[n_in:2 * n_in]
    send_sem, recv_sem, pair_send, pair_recv, local_sem = refs[2 * n_in:]
    place = Place(sizes)
    pos, core = place.pos, place.core
    entry_barrier(place)
    partner = place.device(pos, 1 - core)
    locals_ = []
    for a in range(n_in):
        c = pltpu.make_async_copy(ins[a], outs[a].at[pos["x"], core, pos["z"], pos["y"]], local_sem.at[a])
        c.start()
        locals_.append(c)

    def part(pi, at, who):
        a, tree, lo, n = pieces[pi]
        return outs[a].at[at["x"], who, at["z"], at["y"], pl.ds(lo, n)]

    def remote(src, dst, send, recv, dev):
        return pltpu.make_async_remote_copy(src_ref=src, dst_ref=dst, send_sem=send, recv_sem=recv, device_id=dev, device_id_type=MESH)

    def line(d):
        if sizes[d] == 1:
            return []
        if sizes[d] == 2:
            return [(0, None, 1 - pos[d])]
        return [(0, pos[d] + 1 < sizes[d], pos[d] + 1), (1, pos[d] > 0, pos[d] - 1)]

    left = {}
    for pi, t in order:
        left[pi] = left.get(pi, 0) + 1
    seen = dict.fromkeys(left, 0)
    whole = [slice(None)] * 3
    for pi, t in order:
        a, tree, lo, n = pieces[pi]
        own = all(v == 0 for v in t)
        at, conds = dict(pos), []
        for d, v in zip(tree, t):
            if v == "o":
                at[d] = 1 - pos[d]
            elif v != 0:
                at[d] = pos[d] + v
                conds.append((at[d] >= 0) if v < 0 else (at[d] < sizes[d]))
        chip = place.chip(at)
        dst = part(pi, at, core)
        src = ins[a].at[pl.ds(lo, n)] if own else dst
        k = max([j for j, v in enumerate(t) if v != 0], default=-1)

        def handle(tree=tree, t=t, own=own, chip=chip, dst=dst, src=src, k=k, pi=pi):
            if not own:
                remote(dst, dst, pair_send.at[pi], recv_sem.at[pi, chip], partner).wait_recv()
            for j in (2, 1, 0):
                d = tree[j]
                if j < k:
                    continue
                for slot, ok, q in line(d):
                    if j == k and (t[j] == "o" or (t[j] < 0) != (slot == 0)):
                        continue
                    when([ok], remote(src, dst, send_sem.at[pi, 2 * "xyz".index(d) + slot], recv_sem.at[pi, chip],
                                      place.device({**pos, d: q}, core)).start)
            remote(src, dst, pair_send.at[pi], pair_recv.at[pi], partner).start()
        when(conds, handle)
        seen[pi] += 1

    full = dict.fromkeys("xyz", slice(None))
    for pi, (a, tree, lo, n) in enumerate(pieces):
        for j, d in enumerate(tree):
            at = {e: (slice(None) if tree.index(e) < j else pos[e]) for e in "xyz"}
            for slot, ok, q in line(d):
                sem = send_sem.at[pi, 2 * "xyz".index(d) + slot]
                if sizes[d] == 2:
                    ref = part(pi, at, core)
                    remote(ref, ref, sem, recv_sem.at[pi, 0], partner).wait_send()
                else:
                    for z in range(sizes[d]):
                        ref = part(pi, {**at, d: z}, core)
                        sent = (pos[d] >= z) if slot == 0 else (pos[d] <= z)
                        when([ok, sent], remote(ref, ref, sem, recv_sem.at[pi, 0], partner).wait_send)
        ref = part(pi, full, core)
        remote(ref, ref, pair_send.at[pi], pair_recv.at[pi], partner).wait_send()
        ref = part(pi, full, 1 - core)
        remote(ref, ref, pair_send.at[pi], pair_recv.at[pi], partner).wait_recv()
    for c in locals_:
        c.wait()


def gather_order(sizes, pieces, alpha):
    ev = []
    for pi, (a, tree, lo, n) in enumerate(pieces):
        for t in itertools.product(*[offsets(sizes[d]) for d in tree]):
            hops = sum(1 if v == "o" else abs(v) for v in t)
            ev.append((pi * alpha + hops, pi, t))
    ev.sort(key=lambda e: (e[0], e[1]))
    return [(pi, t) for _, pi, t in ev]


def gather(sizes, shards, alpha=0.05):
    chips = sizes["x"] * sizes["y"] * sizes["z"]
    pieces = []
    for a, s in enumerate(shards):
        tiles = s.shape[0] // 8
        if tiles % 3 == 0 and tiles < 12:
            cuts = [(i, i * tiles // 3, tiles // 3) for i in range(3)]
        elif tiles % 2 == 0:
            cuts = [(i, i * tiles // 2, tiles // 2) for i in range(2)]
        else:
            cuts = [(2, 0, tiles)]
        for tree, lo, n in cuts:
            pieces.append((a, TREES[tree], lo * 8, n * 8))
    order = gather_order(sizes, pieces, alpha)
    n_in = len(shards)
    return pl.pallas_call(
        functools.partial(gather_kernel, sizes, pieces, order, n_in),
        out_shape=[jax.ShapeDtypeStruct((sizes["x"], 2, sizes["z"], sizes["y"]) + s.shape, s.dtype) for s in shards],
        in_specs=[pl.BlockSpec(memory_space=pltpu.VMEM)] * n_in,
        out_specs=[pl.BlockSpec(memory_space=pl.ANY)] * n_in,
        scratch_shapes=[
            pltpu.SemaphoreType.DMA((len(pieces), 6)),
            pltpu.SemaphoreType.DMA((len(pieces), chips)),
            pltpu.SemaphoreType.DMA((len(pieces),)),
            pltpu.SemaphoreType.DMA((len(pieces),)),
            pltpu.SemaphoreType.DMA((n_in,)),
        ],
        compiler_params=pltpu.CompilerParams(collective_id=0, has_side_effects=True),
        name="gather",
    )(*shards)


class View:
    def __init__(self, ref, dims, fixed=None, core=None):
        self.ref, self.dims, self.fixed, self.core = ref, dims, fixed or {}, core

    def fix(self, d, v):
        return View(self.ref, self.dims, {**self.fixed, d: v}, self.core)

    def free(self):
        return [d for d in self.dims if d not in self.fixed]

    def index(self, at, cols=None):
        idx = [self.fixed.get(d, at.get(d, slice(None))) for d in self.dims]
        if self.core is not None:
            core, lo, n = self.core
            return (idx[0], core, *idx[1:], slice(None), pl.ds(lo, n))
        return tuple(idx)

    def whole(self):
        return self.ref.at[self.index({})]


def accumulate(sizes, dst, terms):
    dims = terms[0].free()

    def step(i, carry):
        at = {}
        for d in reversed(dims):
            at[d] = lax.rem(i, sizes[d])
            i = i // sizes[d]
        total = None
        for t in terms:
            v = t.ref[t.index(at)].astype(jnp.float32)
            total = v if total is None else total + v
        if isinstance(dst, View):
            dst.ref[dst.index(at)] = total.astype(dst.ref.dtype)
        else:
            dst(total)
        return carry

    count = 1
    for d in dims:
        count *= sizes[d]
    if count == 1:
        step(0, 0)
    else:
        lax.fori_loop(0, count, step, 0)


def piece_buffers(sizes, piece, rows):
    a, tree, lo, n = piece
    dims = list("xzy")
    shapes = [tuple(sizes[d] for d in dims) + (rows, n)]
    for d in tree:
        dims.remove(d)
        rest = tuple(sizes[e] for e in dims) + (rows, n)
        if sizes[d] == 2:
            shapes.append(rest)
        elif sizes[d] > 2:
            shapes += [(sizes[d],) + rest] * 2
    return shapes


def piece_copies(sizes, tree):
    return 1 + sum(0 if sizes[d] == 1 else 1 if sizes[d] == 2 else 2 * sizes[d] for d in tree)


def piece_events(sizes, tree):
    ev, t = [(0.0, ("pair",))], 0.0
    for j, d in enumerate(tree):
        if sizes[d] == 2:
            t += 1
            ev.append((t, ("swap", j)))
        elif sizes[d] > 2:
            for hop in range(1, sizes[d]):
                for far in range(hop, sizes[d] - 1):
                    dest = sizes[d] - 1 - (far - hop)
                    if dest > hop:
                        ev.append((t + hop + (far - hop) * 0.2, ("up", j, hop, dest)))
                        ev.append((t + hop + (far - hop) * 0.2, ("down", j, sizes[d] - 1 - hop, sizes[d] - 1 - dest)))
            t += sizes[d] - 1
            ev.append((t, ("land", j)))
    return ev


def reduce_kernel(sizes, pieces, order, n_in, *refs):
    ins, outs, rest = refs[:n_in], refs[n_in:2 * n_in], list(refs[2 * n_in:])
    send_sem, recv_sem = rest[-2:]
    place = Place(sizes)
    pos, core = place.pos, place.core
    partner = place.device(pos, 1 - core)
    state, base, sent = [], 0, []
    for pi, (a, tree, lo, n) in enumerate(pieces):
        k = len(piece_buffers(sizes, pieces[pi], 8))
        bufs, rest = rest[:k], rest[k:]
        copies = {"pair": (0, 0)}
        c, b = 1, 1
        for j, d in enumerate(tree):
            if sizes[d] > 1:
                copies[j] = (c, b)
                c += 1 if sizes[d] == 2 else 2 * sizes[d]
                b += 1 if sizes[d] == 2 else 2
        state.append({"bufs": bufs, "base": base, "copies": copies, "cur": None})
        base += c

    def copy(src, dst, sem, dev):
        return pltpu.make_async_remote_copy(src_ref=src, dst_ref=dst, send_sem=send_sem.at[sem], recv_sem=recv_sem.at[sem], device_id=dev, device_id_type=MESH)

    def send(conds, src, dst, sem, dev):
        c = copy(src, dst, sem, dev)
        when(conds, c.start)
        sent.append((conds, c))

    def await_copy(buf, sem):
        copy(buf, buf, sem, partner).wait_recv()

    entry_barrier(place)
    for pi, (a, tree, lo, n) in enumerate(pieces):
        src = View(ins[a], list("xzy"), core=(1 - core, lo, n))
        send([], src.whole(), state[pi]["bufs"][0], state[pi]["base"], partner)

    def launch(pi, j):
        a, tree, lo, n = pieces[pi]
        st = state[pi]
        while j < 3 and sizes[tree[j]] == 1:
            st["cur"] = st["cur"].fix(tree[j], 0)
            j += 1
        if j == 3:
            return
        d, cur = tree[j], st["cur"]
        c, b = st["copies"][j]
        c += st["base"]
        p, size = pos[d], sizes[d]
        if size == 2:
            send([], cur.fix(d, 1 - p).whole(), st["bufs"][b], c, place.device({**pos, d: 1 - p}, core))
            return
        for t in range(size - 1, 0, -1):
            send([p == 0], cur.fix(d, t).whole(), st["bufs"][b].at[t], c + t, place.device({**pos, d: p + 1}, core))
            t = size - 1 - t
            send([p == size - 1], cur.fix(d, t).whole(), st["bufs"][b + 1].at[t], c + size + t, place.device({**pos, d: p - 1}, core))

    def run(pi, what):
        a, tree, lo, n = pieces[pi]
        st = state[pi]
        if what[0] == "pair":
            buf = st["bufs"][0]
            await_copy(buf, st["base"])
            mine = View(ins[a], list("xzy"), core=(core, lo, n))
            st["cur"] = View(buf, list("xzy"))
            accumulate(sizes, st["cur"], [st["cur"], mine])
            launch(pi, 0)
            return
        j = what[1]
        d, cur = tree[j], st["cur"]
        c, b = st["copies"][j]
        c += st["base"]
        p, size = pos[d], sizes[d]
        last = all(sizes[e] == 1 for e in tree[j + 1:])
        left = [e for e in cur.free() if e != d]

        def store(total):
            outs[a][:, pl.ds(lo, n)] = total

        if what[0] == "swap":
            buf = st["bufs"][b]
            await_copy(buf, c)
            new = View(buf, left)
            accumulate(sizes, store if last else new, [cur.fix(d, p), new])
            st["cur"] = new
            launch(pi, j + 1)
        elif what[0] in ("up", "down"):
            up = what[0] == "up"
            here, t = what[2], what[3]
            sem = c + t if up else c + size + t
            buf = st["bufs"][b if up else b + 1]

            def relay():
                await_copy(buf.at[t], sem)
                new = View(buf, [d] + left, {d: t})
                accumulate(sizes, new, [cur.fix(d, t), new])

            when([p == here], relay)
            send([p == here], buf.at[t], buf.at[t], sem, place.device({**pos, d: p + 1 if up else p - 1}, core))
        else:
            ups, downs = st["bufs"][b], st["bufs"][b + 1]
            new = cur.fix(d, p)
            below, above = View(ups, [d] + left, {d: p}), View(downs, [d] + left, {d: p})
            for p_below, p_above, conds in ((False, True, [p == 0]), (True, True, [p > 0, p < size - 1]), (True, False, [p == size - 1])):
                def land(p_below=p_below, p_above=p_above):
                    terms = [new]
                    if p_below:
                        await_copy(ups.at[p], c + p)
                        terms.append(below)
                    if p_above:
                        await_copy(downs.at[p], c + size + p)
                        terms.append(above)
                    accumulate(sizes, store if last else new, terms)
                when(conds, land)
            st["cur"] = new
            launch(pi, j + 1)

    for pi, what in order:
        run(pi, what)
    for conds, c in sent:
        when(conds, c.wait_send)


def reduce_pieces(shapes):
    kinds = itertools.cycle(("xzy", "yzx", "xyz", "xzy", "yzx", "yxz", "xzy", "yzx"))
    pieces = []
    for a, (rows, cols) in enumerate(shapes):
        width = min(cols, max(128, 18432 // rows // 128 * 128))
        while cols % width:
            width -= 128
        pieces += [(a, lo, width) for lo in range(0, cols, width)]
    return [(a, next(kinds), lo, n) for a, lo, n in pieces]


def reduce_scatter(sizes, parts, alpha=0.5):
    shapes = [p.shape[-2:] for p in parts]
    pieces = reduce_pieces(shapes)
    ev = []
    for pi, (a, tree, lo, n) in enumerate(pieces):
        ev += [(pi * alpha + t, pi, what) for t, what in piece_events(sizes, tree)]
    ev.sort(key=lambda e: (e[0], e[1]))
    order = [(pi, what) for _, pi, what in ev]
    buffers, copies = [], 0
    for piece in pieces:
        rows = shapes[piece[0]][0]
        buffers += [pltpu.VMEM(s, parts[piece[0]].dtype) for s in piece_buffers(sizes, piece, rows)]
        copies += piece_copies(sizes, piece[1])
    n_in = len(parts)
    return pl.pallas_call(
        functools.partial(reduce_kernel, sizes, pieces, order, n_in),
        out_shape=[jax.ShapeDtypeStruct(s, jnp.float32) for s in shapes],
        in_specs=[pl.BlockSpec(memory_space=pltpu.VMEM)] * n_in,
        out_specs=[pl.BlockSpec(memory_space=pltpu.VMEM)] * n_in,
        scratch_shapes=buffers + [pltpu.SemaphoreType.DMA((copies,)), pltpu.SemaphoreType.DMA((copies,))],
        compiler_params=pltpu.CompilerParams(collective_id=1, has_side_effects=True, vmem_limit_bytes=67000000),
        name="reduce",
    )(*parts)


HEAD_DIM = 64
PASSES = 4
EPSILON = 1e-05
SCORE_SCALE = 0.125
GELU_COEF = 0.7978845608028654
GELU_CUBE = 0.044715


def dot(left, right, dims=((1,), (0,))):
    return lax.dot_general(left, right, (dims, ((), ())), preferred_element_type=jnp.float32)


NT, TN = ((1,), (1,)), ((0,), (0,))


def normalise(values):
    centre = values - jnp.mean(values, axis=-1, keepdims=True)
    scale = lax.rsqrt(jnp.mean(centre * centre, axis=-1, keepdims=True) + EPSILON)
    return centre * scale, scale


def normalise_back(grad, unit, scale):
    return scale * (grad - jnp.mean(grad, axis=-1, keepdims=True) - unit * jnp.mean(grad * unit, axis=-1, keepdims=True))


def block_kernel(chunk, sections, key_ok, hidden, cotangent, g1, b1, qkv_b, out_b, g2, b2, fc_b, proj_b,
                 qkv_hbm, out_hbm, fc_hbm, proj_hbm,
                 hidden_out, grad_hidden, a_st, o_st, c_st, g_st, dqkv_st, do_st, du_st, dm_st,
                 dg1, db1, dqkv_b, dout_b, dg2, db2, dfc_b, dproj_b,
                 qkv_w, out_w, fc_w, proj_w, state, unit1, unit2, scale1, scale2, qkv_st, prob_st, slope_st, mixed, allow, sems):
    rows, width = hidden.shape
    hidden_width = fc_w.shape[1]
    pair = 2 * HEAD_DIM
    pairs = width // pair
    loads = [pltpu.make_async_copy(src, dst, sems.at[i]) for i, (src, dst) in enumerate(
        ((qkv_hbm, qkv_w), (out_hbm, out_w), (fc_hbm, fc_w), (proj_hbm, proj_w)))]
    for c in loads:
        c.start()
    for ref in (dg1, db1, dqkv_b, dout_b, dg2, db2, dfc_b, dproj_b):
        ref[...] = jnp.zeros_like(ref)
    query = lax.broadcasted_iota(jnp.int32, (rows, 2 * rows), 0)
    key = lax.rem(lax.broadcasted_iota(jnp.int32, (rows, 2 * rows), 1), rows)
    ok = jnp.broadcast_to(key_ok[...], (rows, 2 * rows)) > 0.5
    allow[...] = jnp.where((key < query) & ok | (key == query), 1.0, 0.0)
    state[...] = hidden[...].astype(jnp.float32)
    first = lax.broadcasted_iota(jnp.int32, (rows, pair), 1) < HEAD_DIM

    def both(block):
        wide = block.astype(jnp.float32)
        return jnp.concatenate([jnp.where(first, wide, 0.0), jnp.where(first, 0.0, wide)], axis=0).astype(jnp.bfloat16)

    def merge(block):
        return jnp.where(first, block[:rows], block[rows:])

    def halves(fn, block, *others):
        return [fn(block[:, s], *(o[:, s] for o in others)) for s in (slice(0, rows), slice(rows, 2 * rows))]

    def forward(k, wait):
        x = state[...]
        unit, scale = normalise(x)
        unit1[k] = unit
        scale1[k] = jnp.broadcast_to(scale, scale1.shape[1:])
        a_st[k] = (unit * g1[...] + b1[...]).astype(jnp.bfloat16)
        if wait:
            loads[0].wait()
        for lo in range(0, 3 * width, chunk):
            cols = slice(lo, lo + chunk)
            qkv_st[k, :, cols] = (dot(a_st[k], qkv_w[:, cols]) + qkv_b[:, cols]).astype(jnp.bfloat16)
        for i in range(pairs):
            q = qkv_st[k, :, i * pair:(i + 1) * pair]
            keys = both(qkv_st[k, :, width + i * pair:width + (i + 1) * pair])
            values = both(qkv_st[k, :, 2 * width + i * pair:2 * width + (i + 1) * pair])
            scores = jnp.where(allow[...] > 0.5, dot(q, keys, NT) * SCORE_SCALE, -1e30)

            def softmax(s):
                e = jnp.exp(s - jnp.max(s, axis=-1, keepdims=True))
                return e / jnp.sum(e, axis=-1, keepdims=True)

            probs = jnp.concatenate(halves(softmax, scores), axis=1)
            prob_st[k, i] = probs
            o_st[k, :, i * pair:(i + 1) * pair] = dot(probs.astype(jnp.bfloat16), values).astype(jnp.bfloat16)
        if wait:
            loads[1].wait()
        h = x + (dot(o_st[k], out_w[...]) + out_b[...])
        unit, scale = normalise(h)
        unit2[k] = unit
        scale2[k] = jnp.broadcast_to(scale, scale2.shape[1:])
        c_st[k] = (unit * g2[...] + b2[...]).astype(jnp.bfloat16)
        if wait:
            loads[2].wait()
        for lo in range(0, hidden_width, chunk):
            cols = slice(lo, lo + chunk)
            u = dot(c_st[k], fc_w[:, cols]) + fc_b[:, cols]
            square = u * u
            t = jnp.tanh(GELU_COEF * (u + GELU_CUBE * (square * u)))
            half = 0.5 * (1.0 + t)
            g_st[k, :, cols] = (u * half).astype(jnp.bfloat16)
            slope_st[k, :, cols] = half + 0.5 * u * (1.0 - t * t) * (GELU_COEF * (1.0 + 3.0 * GELU_CUBE * square))
        if wait:
            loads[3].wait()
        y = h + (dot(g_st[k], proj_w[...]) + proj_b[...])

        @pl.when(sections[0] >= k)
        def _():
            state[...] = y

    forward(0, True)
    lax.fori_loop(1, PASSES, lambda k, c: (forward(k, False), c)[1], 0)
    hidden_out[...] = state[...].astype(jnp.bfloat16)
    state[...] = cotangent[...].astype(jnp.float32)

    def column_sums(ref, cols, block):
        ref[:, cols] += jnp.sum(block.astype(jnp.float32), axis=0, keepdims=True)

    def backward(step, carry):
        k = PASSES - 1 - step
        live = (sections[0] >= k).astype(jnp.float32)
        dx = state[...]
        dy = dx * live
        dm_st[k] = dy.astype(jnp.bfloat16)
        column_sums(dproj_b, slice(None), dm_st[k])
        for lo in range(0, hidden_width, chunk):
            cols = slice(lo, lo + chunk)
            du = (dot(dm_st[k], proj_w[cols, :], NT) * slope_st[k, :, cols]).astype(jnp.bfloat16)
            du_st[k, :, cols] = du
            column_sums(dfc_b, cols, du)
        dc = dot(du_st[k], fc_w[...], NT)
        unit = unit2[k]
        dg2[...] += jnp.sum(dc * unit, axis=0, keepdims=True)
        column_sums(db2, slice(None), dc)
        dh = dy + normalise_back(dc * g2[...], unit, scale2[k, :, 0:1])
        state[...] = dh + dx * (1.0 - live)
        do_st[k] = dh.astype(jnp.bfloat16)
        column_sums(dout_b, slice(None), do_st[k])
        mixed[...] = dot(do_st[k], out_w[...], NT).astype(jnp.bfloat16)
        for i in range(pairs):
            at = [slice(j * width + i * pair, j * width + (i + 1) * pair) for j in range(3)]
            q = qkv_st[k, :, at[0]]
            keys, values = both(qkv_st[k, :, at[1]]), both(qkv_st[k, :, at[2]])
            grad = mixed[:, at[0]]
            probs = prob_st[k, i]
            dp = dot(grad, values, NT)

            def scores_back(d, p):
                return p * (d - jnp.sum(d * p, axis=-1, keepdims=True))

            ds = jnp.concatenate(halves(scores_back, dp, probs), axis=1).astype(jnp.bfloat16)
            dv = merge(dot(probs.astype(jnp.bfloat16), grad, TN))
            dq = dot(ds, keys) * SCORE_SCALE
            dk = merge(dot(ds, q, TN)) * SCORE_SCALE
            for j, d in enumerate((dq, dk, dv)):
                dqkv_st[k, :, at[j]] = d.astype(jnp.bfloat16)
        column_sums(dqkv_b, slice(None), dqkv_st[k])
        da = dot(dqkv_st[k], qkv_w[...], NT)
        unit = unit1[k]
        dg1[...] += jnp.sum(da * unit, axis=0, keepdims=True)
        column_sums(db1, slice(None), da)
        state[...] += normalise_back(da * g1[...], unit, scale1[k, :, 0:1])
        return carry

    lax.fori_loop(0, PASSES, backward, 0)
    grad_hidden[...] = state[...]


def run_block(sections, key_valid, hidden, cotangent, attention, mlp):
    g1, b1, qkv_w, qv_b, out_w, out_b = attention
    g2, b2, fc_w, fc_b, proj_w, proj_b = mlp
    rows, width = hidden.shape
    ff = fc_w.shape[1]
    bias = jnp.concatenate([qv_b[:width], jnp.zeros_like(qv_b[:width]), qv_b[width:]])
    vectors = [v.astype(jnp.float32)[None] for v in (g1, b1, bias, out_b, g2, b2, fc_b, proj_b)]
    key_ok = jnp.concatenate([key_valid, key_valid], axis=1).astype(jnp.float32)
    low, high = jnp.bfloat16, jnp.float32
    stacks = [width, width, width, ff, 3 * width, width, ff, width]
    pairs = width // (2 * HEAD_DIM)
    vmem, everywhere = pl.BlockSpec(memory_space=pltpu.VMEM), pl.BlockSpec(memory_space=pl.ANY)
    outs = pl.pallas_call(
        functools.partial(block_kernel, 512 if ff % 512 == 0 and width * 3 % 512 == 0 else 256),
        out_shape=[jax.ShapeDtypeStruct((rows, width), low), jax.ShapeDtypeStruct((rows, width), high)]
        + [jax.ShapeDtypeStruct((PASSES, rows, n), low) for n in stacks]
        + [jax.ShapeDtypeStruct(v.shape, high) for v in vectors],
        in_specs=[pl.BlockSpec(memory_space=pltpu.SMEM)] + [vmem] * 11 + [everywhere] * 4,
        out_specs=[vmem] * 18,
        scratch_shapes=[pltpu.VMEM(w.shape, low) for w in (qkv_w, out_w, fc_w, proj_w)] + [
            pltpu.VMEM((rows, width), high),
            pltpu.VMEM((PASSES, rows, width), high),
            pltpu.VMEM((PASSES, rows, width), high),
            pltpu.VMEM((PASSES, rows, 128), high),
            pltpu.VMEM((PASSES, rows, 128), high),
            pltpu.VMEM((PASSES, rows, 3 * width), low),
            pltpu.VMEM((PASSES, pairs, rows, 2 * rows), high),
            pltpu.VMEM((PASSES, rows, ff), high),
            pltpu.VMEM((rows, width), low),
            pltpu.VMEM((rows, 2 * rows), high),
            pltpu.SemaphoreType.DMA((4,)),
        ],
        compiler_params=pltpu.CompilerParams(vmem_limit_bytes=67000000),
        name="block",
    )(sections, key_ok, hidden, cotangent, *vectors, qkv_w, out_w, fc_w, proj_w)
    hidden_out, grad_hidden = outs[:2]
    a, o, c, g, dqkv, do, du, dm = [s.reshape(PASSES * rows, -1) for s in outs[2:10]]
    dg1, db1, dbias, dout_b, dg2, db2, dfc_b, dproj_b = [v[0] for v in outs[10:]]
    dqv_b = jnp.concatenate([dbias[:width], dbias[2 * width:]])
    factors = ((a, dqkv), (o, do), (c, du), (g, dm))
    return hidden_out, grad_hidden, factors, (dg1, db1, dqv_b, dout_b, dg2, db2, dfc_b, dproj_b)


def fetch_attention(ln1_gain, ln1_bias, qkv_weight, qv_bias, out_weight, out_bias):
    return (
        lax.all_gather(ln1_gain, ("dp", "fsdp"), axis=0, tiled=True),
        lax.all_gather(ln1_bias, ("dp", "fsdp"), axis=0, tiled=True),
        lax.all_gather(qkv_weight, ("dp", "fsdp"), axis=0, tiled=True),
        lax.all_gather(qv_bias, ("dp", "fsdp"), axis=0, tiled=True),
        lax.all_gather(out_weight, ("dp", "fsdp"), axis=0, tiled=True),
        lax.all_gather(out_bias, ("dp", "fsdp"), axis=0, tiled=True),
    )


def fetch_mlp(ln2_gain, ln2_bias, fc_weight, fc_bias, proj_weight, proj_bias):
    return (
        lax.all_gather(ln2_gain, ("dp", "fsdp"), axis=0, tiled=True),
        lax.all_gather(ln2_bias, ("dp", "fsdp"), axis=0, tiled=True),
        lax.all_gather(fc_weight, ("dp", "fsdp"), axis=0, tiled=True),
        lax.all_gather(fc_bias, ("dp", "fsdp"), axis=0, tiled=True),
        lax.all_gather(proj_weight, ("dp", "fsdp"), axis=0, tiled=True),
        lax.all_gather(proj_bias, ("dp", "fsdp"), axis=0, tiled=True),
    )


def fetch_all(sizes, attention, mlp):
    ln1_gain, ln1_bias, qkv_weight, qv_bias, out_weight, out_bias = attention
    ln2_gain, ln2_bias, fc_weight, fc_bias, proj_weight, proj_bias = mlp
    big = (qkv_weight, out_weight, fc_weight, proj_weight)
    small = (ln1_gain, ln1_bias, qv_bias, out_bias, ln2_gain, ln2_bias, fc_bias, proj_bias)
    width = -(-sum(v.shape[0] for v in small) // 1024) * 128
    if any(w.shape[0] % 8 for w in big):
        return fetch_attention(*attention), fetch_mlp(*mlp)
    packed = jnp.concatenate(small)
    packed = jnp.pad(packed, (0, 8 * width - packed.shape[0])).reshape(8, width)
    *full, rows = gather(sizes, (*big, packed))
    qkv_full, out_full, fc_full, proj_full = [w.reshape(-1, w.shape[-1]) for w in full]
    rows = rows.reshape(-1, 8 * width)
    vectors, start = [], 0
    for v in small:
        vectors.append(rows[:, start : start + v.shape[0]].reshape(-1))
        start += v.shape[0]
    g1, b1, qv, ob, g2, b2, fb, pb = vectors
    return (g1, b1, qkv_full, qv, out_full, ob), (g2, b2, fc_full, fb, proj_full, pb)


def sum_all(sizes, factors, vectors):
    chips = sizes["x"] * sizes["y"] * sizes["z"]
    big = [dot(left, right, TN).astype(jnp.bfloat16) for left, right in factors]
    if any(w.shape[0] % (16 * chips) for w in big):
        qkv, out, fc, proj, *sums = [
            lax.psum_scatter(v, ("dp", "fsdp"), scatter_dimension=0, tiled=True).astype(jnp.float32) for v in (*big, *vectors)
        ]
    else:
        lead = (sizes["x"], 2, sizes["z"], sizes["y"])
        rows = jnp.concatenate([v.reshape(2 * chips, -1) for v in vectors], axis=1)
        width = -(-rows.shape[1] // 1024) * 128
        rows = jnp.pad(rows, ((0, 0), (0, 8 * width - rows.shape[1])))
        parts = [w.reshape(*lead, -1, w.shape[1]) for w in big]
        parts.append(rows.reshape(*lead, 8, width))
        qkv, out, fc, proj, packed = reduce_scatter(sizes, parts)
        packed, sums, start = packed.reshape(-1), [], 0
        for v in vectors:
            n = v.shape[0] // (2 * chips)
            sums.append(packed[start : start + n])
            start += n
    g1, b1, qv, ob, g2, b2, fb, pb = sums
    return (g1, b1, qkv, qv, out, ob), (g2, b2, fc, fb, proj, pb)


def body(
    sizes,
    hidden,
    sections,
    lengths,
    token_mask,
    cotangent,
    ln1_gain,
    ln1_bias,
    qkv_weight,
    qv_bias,
    out_weight,
    out_bias,
    ln2_gain,
    ln2_bias,
    fc_weight,
    fc_bias,
    proj_weight,
    proj_bias,
):
    seq_count, seq_len, model_width = hidden.shape
    row_count = seq_count * seq_len
    key_pos = jnp.arange(seq_len, dtype=jnp.int32)
    key_valid = (key_pos[None, :] < lengths[:, None]) & (token_mask == 1)

    current = fetch_all(
        sizes,
        (ln1_gain, ln1_bias, qkv_weight, qv_bias, out_weight, out_bias),
        (ln2_gain, ln2_bias, fc_weight, fc_bias, proj_weight, proj_bias),
    )

    hidden_out, grad_hidden, factors, vectors = run_block(
        sections, key_valid, hidden.reshape(row_count, model_width), cotangent.reshape(row_count, model_width), *current
    )
    attention_grads, finished = sum_all(sizes, factors, vectors)
    hidden_out = hidden_out.reshape(hidden.shape)
    grad_hidden = grad_hidden.reshape(hidden.shape)
    return (
        hidden_out,
        grad_hidden,
        attention_grads[0],
        attention_grads[1],
        attention_grads[2],
        attention_grads[3],
        attention_grads[4],
        attention_grads[5],
        finished[0],
        finished[1],
        finished[2],
        finished[3],
        finished[4],
        finished[5],
    )


def solution(mesh):
    chips_x = mesh.shape["dp"] // 2
    sizes = {"x": chips_x, "y": chips_x, "z": mesh.shape["fsdp"] // chips_x}
    return jax.shard_map(
        functools.partial(body, sizes),
        mesh=mesh,
        in_specs=(
            P(("dp", "fsdp"), None, None),
            P(("dp", "fsdp")),
            P(("dp", "fsdp")),
            P(("dp", "fsdp"), None),
            P(("dp", "fsdp"), None, None),
            P(("dp", "fsdp")),
            P(("dp", "fsdp")),
            P(("dp", "fsdp"), None),
            P(("dp", "fsdp")),
            P(("dp", "fsdp"), None),
            P(("dp", "fsdp")),
            P(("dp", "fsdp")),
            P(("dp", "fsdp")),
            P(("dp", "fsdp"), None),
            P(("dp", "fsdp")),
            P(("dp", "fsdp"), None),
            P(("dp", "fsdp")),
        ),
        out_specs=(
            P(("dp", "fsdp"), None, None),
            P(("dp", "fsdp"), None, None),
            P(("dp", "fsdp")),
            P(("dp", "fsdp")),
            P(("dp", "fsdp"), None),
            P(("dp", "fsdp")),
            P(("dp", "fsdp"), None),
            P(("dp", "fsdp")),
            P(("dp", "fsdp")),
            P(("dp", "fsdp")),
            P(("dp", "fsdp"), None),
            P(("dp", "fsdp")),
            P(("dp", "fsdp"), None),
            P(("dp", "fsdp")),
        ),
        check_vma=False,
    )
```

profile of v0, /device:TPU:0, one launch (start us, length us, event | category | flops | bytes accessed | tf_op | source)
XLA Modules:
  0.0 253.8 jit_solution(8351169331478005084)
XLA Ops:
  0.6 5.4 %concatenate.40 = bf16[288]{0:T(512)(128)(2,1)S(1)} concatenate(bf16[24]{0:T(256)(128)(2,1)} %param.22, bf16[24]{0:T(256)(128)(2,1)} %param.23, bf16[48]{0:T(256)(128)(2,1)} %param.25, bf16[24]{0:T(256)(128)(2,1)} %param.27, bf16[24]{0:T(256)(128)(2,1)} %param.28, bf16[24]{0:T(256)(128)(2,1)} %param.29, bf16[96]{0:T(256)(128)(2,1)} %param.31, bf16[24]{0:T(256)(128)(2,1)} %param.33), dimensions={0} | concatenate | bytes 1152 | tf_op jit(solution)/shard_map/concatenate | solution.py:671
  6.1 0.6 pad_bitcast_fusion.1.refs_4_
  6.7 62.8 %gather.1 = (bf16[2,2,4,2,24,2304]{5,4,3,2,1,0:T(8,128)(2,1)}, bf16[2,2,4,2,24,768]{5,4,3,2,1,0:T(8,128)(2,1)}, bf16[2,2,4,2,24,3072]{5,4,3,2,1,0:T(8,128)(2,1)}...) custom-call(bf16[24,2304]{1,0:T(8,128)(2,1)} %refs_0_.1, bf16[24,768]{1,0:T(8,128)(2,1)} %refs_1_.1, ...), custom_call_target="tpu_custom_call" | custom-call | tf_op jit(solution)/shard_map/gather/pallas_call | solution.py:175
  69.5 0.9 copy.46
  70.4 0.1 fusion.2
  70.4 0.1 concatenate.41
  70.5 0.1 concatenate.42
  70.6 0.6 fusion.1.qkv_b
  71.3 0.1 slice_convert_fusion
  71.3 0.7 reshape.278.g1
  72.0 0.7 reshape.279.b1
  72.7 0.7 reshape.280.out_b
  73.4 0.7 reshape.281.g2
  74.1 0.7 reshape.282.b2
  74.7 0.7 reshape.284.proj_b
  75.4 0.1 slice_convert_fusion.1
  75.5 0.7 reshape.283.fc_b
  76.8 0.7 compare_and_fusion
  77.5 0.6 add_convert_fusion.key_ok
  78.7 50.7 %block.1 = (bf16[128,768]{1,0:T(8,128)(2,1)}, f32[128,768]{1,0:T(8,128)}, bf16[4,128,768]{2,1,0:T(8,128)(2,1)}, bf16[4,128,768]{2,1,0:T(8,128)(2,1)}, bf16[4,128...) custom-call(s32[1]{0:T(128)S(6)} %copy.51.sections, ...), custom_call_target="tpu_custom_call" | custom-call | tf_op jit(solution)/shard_map/block/pallas_call | solution.py:610
  129.4 0.7 slice_reduce_fusion.1
  130.1 0.1 concatenate.44
  130.2 0.1 concatenate.45
  130.3 0.5 broadcast.32
  130.8 1.4 reduce.14
  132.2 0.1 reshape_squeeze.26
  132.3 0.7 reduce.1
  133.0 0.1 reshape_squeeze.21
  133.1 0.7 reduce.2
  133.8 0.1 reshape_squeeze.22
  133.8 0.7 reduce.5
  134.5 0.1 reshape_squeeze.23
  134.6 0.7 reduce.6
  135.3 0.1 reshape_squeeze.24
  135.4 0.7 reduce.7
  136.1 0.1 reshape_squeeze.25
  136.2 0.7 reduce.9
  136.9 0.1 reshape_squeeze.27
  137.0 0.1 concatenate.47
  137.1 0.7 copy.44
  137.8 0.0 copy-start
  137.8 0.0 copy-start.5
  137.8 7.0 %bitcast_convert_fusion = bf16[3072,768]{1,0:T(8,128)(2,1)} fusion(bf16[4,128,3072]{2,1,0:T(8,128)(2,1)} %get-tuple-element.55, bf16[4,128,768]{2,1,0:T(8,128)(2,1)} %get-tuple-element.56), kind=kOutput, calls=%fused_computation | convolution fusion | flops 2418278400 | bytes 8650752 | tf_op jit(solution)/shard_map/dot_general | solution.py:443
  144.8 0.0 copy-done
  144.8 0.0 copy-done.5
  144.8 0.0 copy-start.3
  144.8 0.0 copy-start.4
  144.8 4.7 %bitcast_convert_fusion.1 = bf16[768,3072]{1,0:T(8,128)(2,1)} fusion(bf16[4,128,768]{2,1,0:T(8,128)(2,1)S(1)} %copy-done.5, bf16[4,128,3072]{2,1,0:T(8,128)(2,1)S(1)} %copy-done), kind=kOutput, calls=%fused_computation.1 | convolution fusion | flops 2418278400 | bytes 8650752 | tf_op jit(solution)/shard_map/dot_general | solution.py:443
  149.5 0.0 copy-start.1
  149.5 0.0 copy-start.2
  149.5 0.0 copy-done.3
  149.5 0.0 copy-done.4
  149.5 1.9 bitcast_convert_fusion.3
  151.3 0.0 copy-done.1
  151.3 0.2 copy-done.2
  151.6 3.8 %bitcast_convert_fusion.2 = bf16[768,2304]{1,0:T(8,128)(2,1)} fusion(bf16[4,128,768]{2,1,0:T(8,128)(2,1)S(1)} %copy-done.2, bf16[4,128,2304]{2,1,0:T(8,128)(2,1)S(1)} %copy-done.1), kind=kOutput, calls=%fused_computation.2 | convolution fusion | flops 1813708800 | bytes 6684672 | tf_op jit(solution)/shard_map/dot_general | solution.py:443
  155.4 87.8 %reduce.15 = (f32[24,2304]{1,0:T(8,128)}, f32[24,768]{1,0:T(8,128)}, f32[24,3072]{1,0:T(8,128)}, f32[96,768]{1,0:T(8,128)}, f32[8,128]{1,0:T(8,128)}) custom-call(bf16[2,2,4,2,24,2304]{5,4,3,2,1,0:T(8,128)(2,1)} %bitcast.46, bf16[2,2,4,2,24,768]{5,4,3,2,1,0:T(8,128)(2,1)} %bitcast.48, bf16[2,2,4,2,24,3072]{5,4,3,2,1,0:T(8,128)(2,1)} %bitcast.43, ...), custom_call_target="tpu_custom_call" | custom-call | tf_op jit(solution)/shard_map/reduce/pallas_call | solution.py:423
  243.2 1.5 fusion.3
  244.7 1.3 slice.77
  246.0 1.3 slice.81
  247.2 1.6 copy.53
  248.9 1.5 copy.54
  250.4 1.7 copy.55
  252.1 1.7 copy.56
  (4 shorter events, 0.0 us)
Async XLA Ops:
  137.8 7.0 %copy-start = (bf16[4,128,3072]{2,1,0:T(8,128)(2,1)S(1)}, bf16[4,128,3072]{2,1,0:T(8,128)(2,1)}, u32[]{:S(2)}) copy-start(bf16[4,128,3072]{2,1,0:T(8,128)(2,1)} %get-tuple-element.54) | copy-start | bytes 9437188
  137.8 7.0 %copy-start.5 = (bf16[4,128,768]{2,1,0:T(8,128)(2,1)S(1)}, bf16[4,128,768]{2,1,0:T(8,128)(2,1)}, u32[]{:S(2)}) copy-start(bf16[4,128,768]{2,1,0:T(8,128)(2,1)} %get-tuple-element.53) | copy-start | bytes 2359300
  144.8 4.7 %copy-start.3 = (bf16[4,128,768]{2,1,0:T(8,128)(2,1)S(1)}, bf16[4,128,768]{2,1,0:T(8,128)(2,1)}, u32[]{:S(2)}) copy-start(bf16[4,128,768]{2,1,0:T(8,128)(2,1)} %get-tuple-element.51) | copy-start | bytes 2359300
  144.8 4.7 %copy-start.4 = (bf16[4,128,768]{2,1,0:T(8,128)(2,1)S(1)}, bf16[4,128,768]{2,1,0:T(8,128)(2,1)}, u32[]{:S(2)}) copy-start(bf16[4,128,768]{2,1,0:T(8,128)(2,1)} %get-tuple-element.52) | copy-start | bytes 2359300
  149.5 1.9 copy-start.1
  149.5 2.1 copy-start.2
where the time goes:
time: 255 us; the launch traced here: 254 us
  Pallas kernels  201 us (79%)
  local copies, waits for them, and re-layouts  25.4 us (10%)
  matrix products  17.4 us (7%)
  other arithmetic  7.56 us (3%)
    pallas_call x1, Pallas kernels, reduce_scatter(): pl.pallas_call(functools.partial(reduce_kernel, sizes, pieces, order, n_i...  87.8 us
    pallas_call x1, Pallas kernels, gather(): pl.pallas_call(functools.partial(gather_kernel, sizes, pieces, order, n_i...  62.8 us
    pallas_call x1, Pallas kernels, run_block(): pl.pallas_call(functools.partial(block_kernel, 512 if ff % 512 == 0 and w...  50.7 us
    dot_general x4, matrix products, dot(): lax.dot_general(left, right, (dims, ((), ())), preferred_element_type=jnp...  17.4 us
    unnamed x19, local copies, waits for them, and re-layouts  8.33 us
    pallas_call x7, other arithmetic, run_block(): pl.pallas_call(functools.partial(block_kernel, 512 if ff % 512 == 0 and w...  5.53 us
    concatenate x1, local copies, waits for them, and re-layouts, fetch_all(): packed = jnp.concatenate(small)  5.43 us

commit v1 on v0

--- a/solution.py
+++ b/solution.py
@@ -1,4 +1,5 @@
 import functools
+import heapq
 import itertools
 
 import jax
@@ -255,27 +256,96 @@
     return 1 + sum(0 if sizes[d] == 1 else 1 if sizes[d] == 2 else 2 * sizes[d] for d in tree)
 
 
-def piece_events(sizes, tree):
-    ev, t = [(0.0, ("pair",))], 0.0
-    for j, d in enumerate(tree):
-        if sizes[d] == 2:
-            t += 1
-            ev.append((t, ("swap", j)))
-        elif sizes[d] > 2:
-            for hop in range(1, sizes[d]):
-                for far in range(hop, sizes[d] - 1):
-                    dest = sizes[d] - 1 - (far - hop)
-                    if dest > hop:
-                        ev.append((t + hop + (far - hop) * 0.2, ("up", j, hop, dest)))
-                        ev.append((t + hop + (far - hop) * 0.2, ("down", j, sizes[d] - 1 - hop, sizes[d] - 1 - dest)))
-            t += sizes[d] - 1
-            ev.append((t, ("land", j)))
-    return ev
-
-
-def reduce_kernel(sizes, pieces, order, n_in, *refs):
-    ins, outs, rest = refs[:n_in], refs[n_in:2 * n_in], list(refs[2 * n_in:])
+def tree_loads(sizes, tree):
+    share, loads = 1.0, {}
+    for d in tree:
+        loads[d] = share * (sizes[d] - 1) / sizes[d]
+        share /= sizes[d]
+    return loads
+
+
+def cut(shapes):
+    order = sorted(range(len(shapes)), key=lambda a: -shapes[a][0] * shapes[a][1])
+    out = []
+    for i, a in enumerate(order):
+        rows, cols = shapes[a]
+        wide = max(256, 18432 // rows // 256 * 256)
+        lo, small = 0, [256, 512] if i == 0 else [256] * 9 if i == len(order) - 1 else []
+        while lo < cols:
+            n = min(small.pop(0) if small else wide, cols - lo)
+            out.append((a, lo, n))
+            lo += n
+    return out
+
+
+def plan(sizes, shapes, rates):
+    make_us, pair_us, link_us, hop_us = rates
+    used, pieces, size = dict.fromkeys("xyz", 0.0), [], {}
+    for a, lo, n in cut(shapes):
+        rows = shapes[a][0]
+        units = rows * n / 6144
+
+        def worst(tree):
+            loads = tree_loads(sizes, tree)
+            return max(used[d] + units * loads[d] for d in tree), used[tree[0]]
+
+        tree = min(("xzy", "yzx", "xyz", "yxz"), key=worst)
+        for d, v in tree_loads(sizes, tree).items():
+            used[d] += units * v
+        size[len(pieces)] = units
+        pieces.append((a, tree, lo, n))
+    order, free, heap, count = [], dict.fromkeys(("pair", "x", "y", "z"), 0.0), [], itertools.count()
+    now = 0.0
+
+    def push(t, pi, what):
+        heapq.heappush(heap, (t, next(count), pi, what))
+
+    def carry(link, t, us):
+        free[link] = max(t, free[link]) + us
+        return free[link] + hop_us
+
+    def launch(t, pi, j):
+        tree = pieces[pi][1]
+        if j == 3:
+            return
+        d = tree[j]
+        part = size[pi]
+        for e in tree[:j + 1]:
+            part /= sizes[e]
+        if sizes[d] == 1:
+            launch(t, pi, j + 1)
+        elif sizes[d] == 2:
+            push(carry(d, t, part * link_us), pi, ("swap", j))
+        else:
+            top = sizes[d] - 1
+            arrive = [carry(d, t, part * link_us) for _ in range(top)]
+            for hop in range(1, top):
+                for dest in range(top, hop, -1):
+                    when_us = arrive[top - dest] + (hop - 1) * (hop_us + part * link_us)
+                    push(when_us, pi, ("up", j, hop, dest))
+                    push(when_us, pi, ("down", j, top - hop, top - dest))
+            push(arrive[-1] + (top - 1) * hop_us + part * link_us, pi, ("land", j))
+
+    for pi in range(len(pieces)):
+        now += make_us * size[pi]
+        push(now, pi, ("make",))
+    while heap:
+        t, _, pi, what = heapq.heappop(heap)
+        order.append((pi, what))
+        if what[0] == "make":
+            push(carry("pair", t, size[pi] / 2 * pair_us), pi, ("pair",))
+        elif what[0] == "pair":
+            launch(t, pi, 0)
+        elif what[0] in ("swap", "land"):
+            launch(t, pi, what[1] + 1)
+    return pieces, order
+
+
+def reduce_kernel(sizes, pieces, order, weights, *refs):
+    lefts, rights, packed = refs[:weights], refs[weights:2 * weights], refs[2 * weights]
+    outs, rest = refs[2 * weights + 1:3 * weights + 2], list(refs[3 * weights + 2:])
     send_sem, recv_sem = rest[-2:]
+    ins, rest = [*rest[:weights], packed], rest[weights:]
     place = Place(sizes)
     pos, core = place.pos, place.core
     partner = place.device(pos, 1 - core)
@@ -305,9 +375,17 @@
         copy(buf, buf, sem, partner).wait_recv()
 
     entry_barrier(place)
-    for pi, (a, tree, lo, n) in enumerate(pieces):
-        src = View(ins[a], list("xzy"), core=(1 - core, lo, n))
-        send([], src.whole(), state[pi]["bufs"][0], state[pi]["base"], partner)
+
+    def make(a, lo, n):
+        total, rows = lefts[a].shape[0], ins[a].shape[4]
+        places = list(itertools.product(*[range(v) for v in ins[a].shape[:4]]))
+        step = min(total, 768)
+        for top in range(0, total, step):
+            for left in range(lo, lo + n, 256):
+                cols = slice(left, min(left + 256, lo + n))
+                block = dot(lefts[a][top:top + step, :], rights[a][:, cols]).astype(ins[a].dtype)
+                for i in range(step // rows):
+                    ins[a][(*places[top // rows + i], slice(None), cols)] = block[i * rows:(i + 1) * rows]
 
     def launch(pi, j):
         a, tree, lo, n = pieces[pi]
@@ -332,6 +410,12 @@
     def run(pi, what):
         a, tree, lo, n = pieces[pi]
         st = state[pi]
+        if what[0] == "make":
+            if a < weights:
+                make(a, lo, n)
+            src = View(ins[a], list("xzy"), core=(1 - core, lo, n))
+            send([], src.whole(), st["bufs"][0], st["base"], partner)
+            return
         if what[0] == "pair":
             buf = st["bufs"][0]
             await_copy(buf, st["base"])
@@ -395,40 +479,58 @@
         when(conds, c.wait_send)
 
 
-def reduce_pieces(shapes):
-    kinds = itertools.cycle(("xzy", "yzx", "xyz", "xzy", "yzx", "yxz", "xzy", "yzx"))
-    pieces = []
-    for a, (rows, cols) in enumerate(shapes):
-        width = min(cols, max(128, 18432 // rows // 128 * 128))
-        while cols % width:
-            width -= 128
-        pieces += [(a, lo, width) for lo in range(0, cols, width)]
-    return [(a, next(kinds), lo, n) for a, lo, n in pieces]
-
-
-def reduce_scatter(sizes, parts, alpha=0.5):
-    shapes = [p.shape[-2:] for p in parts]
-    pieces = reduce_pieces(shapes)
-    ev = []
-    for pi, (a, tree, lo, n) in enumerate(pieces):
-        ev += [(pi * alpha + t, pi, what) for t, what in piece_events(sizes, tree)]
-    ev.sort(key=lambda e: (e[0], e[1]))
-    order = [(pi, what) for _, pi, what in ev]
+def reduce_scatter(sizes, factors, packed, rates=(0.3, 1.2, 4.3, 1.2)):
+    chips = sizes["x"] * sizes["y"] * sizes["z"]
+    lead = (sizes["x"], 2, sizes["z"], sizes["y"])
+    low = [(left.shape[0] // (2 * chips), right.shape[1]) for left, right in factors]
+    shapes = low + [packed.shape[-2:]]
+    pieces, order = plan(sizes, shapes, rates)
     buffers, copies = [], 0
     for piece in pieces:
-        rows = shapes[piece[0]][0]
-        buffers += [pltpu.VMEM(s, parts[piece[0]].dtype) for s in piece_buffers(sizes, piece, rows)]
+        kind = jnp.bfloat16 if piece[0] < len(low) else packed.dtype
+        buffers += [pltpu.VMEM(s, kind) for s in piece_buffers(sizes, piece, shapes[piece[0]][0])]
         copies += piece_copies(sizes, piece[1])
-    n_in = len(parts)
+    vmem = pl.BlockSpec(memory_space=pltpu.VMEM)
     return pl.pallas_call(
-        functools.partial(reduce_kernel, sizes, pieces, order, n_in),
+        functools.partial(reduce_kernel, sizes, pieces, order, len(low)),
         out_shape=[jax.ShapeDtypeStruct(s, jnp.float32) for s in shapes],
-        in_specs=[pl.BlockSpec(memory_space=pltpu.VMEM)] * n_in,
-        out_specs=[pl.BlockSpec(memory_space=pltpu.VMEM)] * n_in,
-        scratch_shapes=buffers + [pltpu.SemaphoreType.DMA((copies,)), pltpu.SemaphoreType.DMA((copies,))],
+        in_specs=[vmem] * (2 * len(low) + 1),
+        out_specs=[vmem] * len(shapes),
+        scratch_shapes=[pltpu.VMEM(lead + s, jnp.bfloat16) for s in low] + buffers
+        + [pltpu.SemaphoreType.DMA((copies,)), pltpu.SemaphoreType.DMA((copies,))],
         compiler_params=pltpu.CompilerParams(collective_id=1, has_side_effects=True, vmem_limit_bytes=67000000),
         name="reduce",
-    )(*parts)
+    )(*[left for left, _ in factors], *[right for _, right in factors], packed)
+
+
+def finish_kernel(chunks, packed, *refs):
+    n = (len(refs) - 1 - len(chunks)) // 3
+    ins, outs, vectors, bufs, sems = refs[:n], refs[n:2 * n], refs[2 * n:2 * n + len(chunks)], refs[2 * n + len(chunks):-1], refs[-1]
+    loads = [pltpu.make_async_copy(a, b, sems.at[0, i]) for i, (a, b) in enumerate(zip(ins, bufs))]
+    stores = [pltpu.make_async_copy(b, o, sems.at[1, i]) for i, (b, o) in enumerate(zip(bufs, outs))]
+    for c in loads:
+        c.start()
+    for i, w in enumerate(chunks):
+        vectors[i][...] = packed[i:i + 1, :w]
+    for c, o in zip(loads, stores):
+        c.wait()
+        o.start()
+    for o in stores:
+        o.wait()
+
+
+def finish(chunks, arrays, packed):
+    n = len(arrays)
+    vmem, everywhere = pl.BlockSpec(memory_space=pltpu.VMEM), pl.BlockSpec(memory_space=pl.ANY)
+    out = pl.pallas_call(
+        functools.partial(finish_kernel, chunks),
+        out_shape=[jax.ShapeDtypeStruct(a.shape, a.dtype) for a in arrays] + [jax.ShapeDtypeStruct((1, w), packed.dtype) for w in chunks],
+        in_specs=[vmem] + [everywhere] * n,
+        out_specs=[everywhere] * n + [vmem] * len(chunks),
+        scratch_shapes=[pltpu.VMEM(a.shape, a.dtype) for a in arrays] + [pltpu.SemaphoreType.DMA((2, n))],
+        name="finish",
+    )(packed, *arrays)
+    return out[:n], [v[0] for v in out[n:]]
 
 
 HEAD_DIM = 64
@@ -458,9 +560,9 @@
 
 def block_kernel(chunk, sections, key_ok, hidden, cotangent, g1, b1, qkv_b, out_b, g2, b2, fc_b, proj_b,
                  qkv_hbm, out_hbm, fc_hbm, proj_hbm,
-                 hidden_out, grad_hidden, a_st, o_st, c_st, g_st, dqkv_st, do_st, du_st, dm_st,
+                 hidden_out, grad_hidden, a_t, o_t, c_t, g_t, dqkv_st, do_st, du_st, dm_st,
                  dg1, db1, dqkv_b, dout_b, dg2, db2, dfc_b, dproj_b,
-                 qkv_w, out_w, fc_w, proj_w, state, unit1, unit2, scale1, scale2, qkv_st, prob_st, slope_st, mixed, allow, sems):
+                 qkv_w, out_w, fc_w, proj_w, state, unit1, unit2, scale1, scale2, qkv_st, prob_st, slope_st, mixed, wide, allow, sems):
     rows, width = hidden.shape
     hidden_width = fc_w.shape[1]
     pair = 2 * HEAD_DIM
@@ -493,12 +595,15 @@
         unit, scale = normalise(x)
         unit1[k] = unit
         scale1[k] = jnp.broadcast_to(scale, scale1.shape[1:])
-        a_st[k] = (unit * g1[...] + b1[...]).astype(jnp.bfloat16)
+        at = pl.ds(pl.multiple_of(k * rows, rows), rows)
+        a = (unit * g1[...] + b1[...]).astype(jnp.bfloat16)
+        mixed[...] = a
+        a_t[:, at] = a.T
         if wait:
             loads[0].wait()
         for lo in range(0, 3 * width, chunk):
             cols = slice(lo, lo + chunk)
-            qkv_st[k, :, cols] = (dot(a_st[k], qkv_w[:, cols]) + qkv_b[:, cols]).astype(jnp.bfloat16)
+            qkv_st[k, :, cols] = (dot(mixed[...], qkv_w[:, cols]) + qkv_b[:, cols]).astype(jnp.bfloat16)
         for i in range(pairs):
             q = qkv_st[k, :, i * pair:(i + 1) * pair]
             keys = both(qkv_st[k, :, width + i * pair:width + (i + 1) * pair])
@@ -511,27 +616,33 @@
 
             probs = jnp.concatenate(halves(softmax, scores), axis=1)
             prob_st[k, i] = probs
-            o_st[k, :, i * pair:(i + 1) * pair] = dot(probs.astype(jnp.bfloat16), values).astype(jnp.bfloat16)
+            o = dot(probs.astype(jnp.bfloat16), values).astype(jnp.bfloat16)
+            mixed[:, i * pair:(i + 1) * pair] = o
+            o_t[i * pair:(i + 1) * pair, at] = o.T
         if wait:
             loads[1].wait()
-        h = x + (dot(o_st[k], out_w[...]) + out_b[...])
+        h = x + (dot(mixed[...], out_w[...]) + out_b[...])
         unit, scale = normalise(h)
         unit2[k] = unit
         scale2[k] = jnp.broadcast_to(scale, scale2.shape[1:])
-        c_st[k] = (unit * g2[...] + b2[...]).astype(jnp.bfloat16)
+        c = (unit * g2[...] + b2[...]).astype(jnp.bfloat16)
+        mixed[...] = c
+        c_t[:, at] = c.T
         if wait:
             loads[2].wait()
         for lo in range(0, hidden_width, chunk):
             cols = slice(lo, lo + chunk)
-            u = dot(c_st[k], fc_w[:, cols]) + fc_b[:, cols]
+            u = dot(mixed[...], fc_w[:, cols]) + fc_b[:, cols]
             square = u * u
             t = jnp.tanh(GELU_COEF * (u + GELU_CUBE * (square * u)))
             half = 0.5 * (1.0 + t)
-            g_st[k, :, cols] = (u * half).astype(jnp.bfloat16)
+            g = (u * half).astype(jnp.bfloat16)
+            wide[:, cols] = g
+            g_t[cols, at] = g.T
             slope_st[k, :, cols] = half + 0.5 * u * (1.0 - t * t) * (GELU_COEF * (1.0 + 3.0 * GELU_CUBE * square))
         if wait:
             loads[3].wait()
-        y = h + (dot(g_st[k], proj_w[...]) + proj_b[...])
+        y = h + (dot(wide[...], proj_w[...]) + proj_b[...])
 
         @pl.when(sections[0] >= k)
         def _():
@@ -604,13 +715,14 @@
     vectors = [v.astype(jnp.float32)[None] for v in (g1, b1, bias, out_b, g2, b2, fc_b, proj_b)]
     key_ok = jnp.concatenate([key_valid, key_valid], axis=1).astype(jnp.float32)
     low, high = jnp.bfloat16, jnp.float32
-    stacks = [width, width, width, ff, 3 * width, width, ff, width]
+    lefts, rights = [width, width, width, ff], [3 * width, width, ff, width]
     pairs = width // (2 * HEAD_DIM)
     vmem, everywhere = pl.BlockSpec(memory_space=pltpu.VMEM), pl.BlockSpec(memory_space=pl.ANY)
     outs = pl.pallas_call(
         functools.partial(block_kernel, 512 if ff % 512 == 0 and width * 3 % 512 == 0 else 256),
         out_shape=[jax.ShapeDtypeStruct((rows, width), low), jax.ShapeDtypeStruct((rows, width), high)]
-        + [jax.ShapeDtypeStruct((PASSES, rows, n), low) for n in stacks]
+        + [jax.ShapeDtypeStruct((n, PASSES * rows), low) for n in lefts]
+        + [jax.ShapeDtypeStruct((PASSES, rows, n), low) for n in rights]
         + [jax.ShapeDtypeStruct(v.shape, high) for v in vectors],
         in_specs=[pl.BlockSpec(memory_space=pltpu.SMEM)] + [vmem] * 11 + [everywhere] * 4,
         out_specs=[vmem] * 18,
@@ -624,6 +736,7 @@
             pltpu.VMEM((PASSES, pairs, rows, 2 * rows), high),
             pltpu.VMEM((PASSES, rows, ff), high),
             pltpu.VMEM((rows, width), low),
+            pltpu.VMEM((rows, ff), low),
             pltpu.VMEM((rows, 2 * rows), high),
             pltpu.SemaphoreType.DMA((4,)),
         ],
@@ -631,7 +744,8 @@
         name="block",
     )(sections, key_ok, hidden, cotangent, *vectors, qkv_w, out_w, fc_w, proj_w)
     hidden_out, grad_hidden = outs[:2]
-    a, o, c, g, dqkv, do, du, dm = [s.reshape(PASSES * rows, -1) for s in outs[2:10]]
+    a, o, c, g = outs[2:6]
+    dqkv, do, du, dm = [s.reshape(PASSES * rows, -1) for s in outs[6:10]]
     dg1, db1, dbias, dout_b, dg2, db2, dfc_b, dproj_b = [v[0] for v in outs[10:]]
     dqv_b = jnp.concatenate([dbias[:width], dbias[2 * width:]])
     factors = ((a, dqkv), (o, do), (c, du), (g, dm))
@@ -683,24 +797,19 @@
 
 def sum_all(sizes, factors, vectors):
     chips = sizes["x"] * sizes["y"] * sizes["z"]
-    big = [dot(left, right, TN).astype(jnp.bfloat16) for left, right in factors]
-    if any(w.shape[0] % (16 * chips) for w in big):
+    if any(left.shape[0] % (16 * chips) for left, _ in factors):
+        big = [dot(left, right).astype(jnp.bfloat16) for left, right in factors]
         qkv, out, fc, proj, *sums = [
             lax.psum_scatter(v, ("dp", "fsdp"), scatter_dimension=0, tiled=True).astype(jnp.float32) for v in (*big, *vectors)
         ]
     else:
         lead = (sizes["x"], 2, sizes["z"], sizes["y"])
-        rows = jnp.concatenate([v.reshape(2 * chips, -1) for v in vectors], axis=1)
-        width = -(-rows.shape[1] // 1024) * 128
-        rows = jnp.pad(rows, ((0, 0), (0, 8 * width - rows.shape[1])))
-        parts = [w.reshape(*lead, -1, w.shape[1]) for w in big]
-        parts.append(rows.reshape(*lead, 8, width))
-        qkv, out, fc, proj, packed = reduce_scatter(sizes, parts)
-        packed, sums, start = packed.reshape(-1), [], 0
-        for v in vectors:
-            n = v.shape[0] // (2 * chips)
-            sums.append(packed[start : start + n])
-            start += n
+        chunks = [v.shape[0] // (2 * chips) for v in vectors]
+        width = -(-max(chunks) // 128) * 128
+        rows = [jnp.pad(v.reshape(2 * chips, 1, w), ((0, 0), (0, 0), (0, width - w))) for v, w in zip(vectors, chunks)]
+        packed = jnp.concatenate(rows, axis=1).reshape(*lead, 8, width)
+        *big, packed = reduce_scatter(sizes, factors, packed)
+        (qkv, out, fc, proj), sums = finish(chunks, big, packed)
     g1, b1, qv, ob, g2, b2, fb, pb = sums
     return (g1, b1, qkv, qv, out, ob), (g2, b2, fc, fb, proj, pb)
 

time: 255 us -> 226 us (0.89)
  matrix products: 17.4 us -> 0 us
  local copies, waits for them, and re-layouts: 25.4 us -> 14.6 us
    dot_general x4 -> x0, matrix products: 17.4 us -> none  [dot(): lax.dot_general(left, right, (dims, ((), ())), preferred_element_type=jnp...]
    unnamed x19 -> x7, local copies, waits for them, and re-layouts: 8.33 us -> 0.89 us
    slice x3 -> x0, local copies, waits for them, and re-layouts: 4.01 us -> none  [sum_all(): sums.append(packed[start:start + n])]
    pallas_call x1 -> x2, Pallas kernels: 87.8 us -> 86.2 us  [the longest x1 82.9 us: reduce_scatter(): pl.pallas_call(functools.partial(reduce_kernel, sizes, pieces, order, len...]
where the time goes in v1:
time: 226 us
  Pallas kernels  201 us (89%)
  local copies, waits for them, and re-layouts  14.6 us (6%)
  other arithmetic  7.56 us (3%)
  between operations  2.32 us (1%)
    pallas_call x1, Pallas kernels, reduce_scatter(): pl.pallas_call(functools.partial(reduce_kernel, sizes, pieces, order, len...  82.9 us
    pallas_call x1, Pallas kernels, gather(): pl.pallas_call(functools.partial(gather_kernel, sizes, pieces, order, n_i...  62.8 us
    pallas_call x1, Pallas kernels, run_block(): pl.pallas_call(functools.partial(block_kernel, 512 if ff % 512 == 0 and w...  52.2 us
    pallas_call x7, other arithmetic, run_block(): pl.pallas_call(functools.partial(block_kernel, 512 if ff % 512 == 0 and w...  5.53 us
    concatenate x1, local copies, waits for them, and re-layouts, fetch_all(): packed = jnp.concatenate(small)  5.43 us
    convert_element_type x7, local copies, waits for them, and re-layouts, run_block(): v.astype(jnp.float32)[None]  4.76 us

profile of v1, /device:TPU:0, one launch (start us, length us, event | category | flops | bytes accessed | tf_op | source)
XLA Modules:
  0.0 225.6 jit_solution(4681128908042626724)
XLA Ops:
  0.6 5.4 %concatenate.40 = bf16[288]{0:T(512)(128)(2,1)S(1)} concatenate(bf16[24]{0:T(256)(128)(2,1)} %param.22, bf16[24]{0:T(256)(128)(2,1)} %param.23, bf16[48]{0:T(256)(128)(2,1)} %param.25, bf16[24]{0:T(256)(128)(2,1)} %param.27, bf16[24]{0:T(256)(128)(2,1)} %param.28, bf16[24]{0:T(256)(128)(2,1)} %param.29, bf16[96]{0:T(256)(128)(2,1)} %param.31, bf16[24]{0:T(256)(128)(2,1)} %param.33), dimensions={0} | concatenate | bytes 1152 | tf_op jit(solution)/shard_map/concatenate | solution.py:785
  6.1 0.6 pad_bitcast_fusion.refs_4_
  6.7 62.8 %gather.1 = (bf16[2,2,4,2,24,2304]{5,4,3,2,1,0:T(8,128)(2,1)}, bf16[2,2,4,2,24,768]{5,4,3,2,1,0:T(8,128)(2,1)}, bf16[2,2,4,2,24,3072]{5,4,3,2,1,0:T(8,128)(2,1)}...) custom-call(bf16[24,2304]{1,0:T(8,128)(2,1)} %refs_0_.1, bf16[24,768]{1,0:T(8,128)(2,1)} %refs_1_.1, ...), custom_call_target="tpu_custom_call" | custom-call | tf_op jit(solution)/shard_map/gather/pallas_call | solution.py:176
  69.5 0.9 copy.43
  70.4 0.1 fusion.2
  70.4 0.1 concatenate.41
  70.5 0.1 concatenate.42
  70.6 0.6 fusion.1.qkv_b
  71.3 0.1 slice_convert_fusion
  71.3 0.7 reshape.266.g1
  72.0 0.7 reshape.267.b1
  72.7 0.7 reshape.268.out_b
  73.4 0.7 reshape.269.g2
  74.1 0.7 reshape.270.b2
  74.7 0.7 reshape.272.proj_b
  75.4 0.1 slice_convert_fusion.1
  75.5 0.7 reshape.271.fc_b
  76.8 0.7 compare_and_fusion
  77.5 0.6 add_convert_fusion.key_ok
  78.7 52.2 %block.1 = (bf16[128,768]{1,0:T(8,128)(2,1)}, f32[128,768]{1,0:T(8,128)}, bf16[768,512]{1,0:T(8,128)(2,1)}, bf16[768,512]{1,0:T(8,128)(2,1)}, bf16[768,512]{1,0:...) custom-call(s32[1]{0:T(128)S(6)} %copy.51.sections, ...), custom_call_target="tpu_custom_call" | custom-call | tf_op jit(solution)/shard_map/block/pallas_call | solution.py:721
  130.9 0.7 reduce.1
  131.6 0.1 reshape_squeeze.21
  131.7 0.7 reduce.2
  132.4 0.1 reshape_squeeze.22
  132.5 0.7 slice_reduce_fusion.1
  133.2 0.1 concatenate.44
  133.3 0.1 concatenate.45
  133.4 0.7 reduce.5
  134.1 0.1 reshape_squeeze.23
  134.2 0.7 reduce.6
  134.9 0.1 reshape_squeeze.24
  135.0 0.7 reduce.7
  135.7 0.1 reshape_squeeze.25
  135.8 0.5 broadcast.52
  136.3 1.4 reduce.14
  137.7 0.1 reshape_squeeze.26
  137.8 0.7 reduce.9
  138.4 0.1 reshape_squeeze.27
  138.5 0.7 copy.40
  139.3 82.9 %reduce.15 = (f32[24,2304]{1,0:T(8,128)}, f32[24,768]{1,0:T(8,128)}, f32[24,3072]{1,0:T(8,128)}, f32[96,768]{1,0:T(8,128)}, f32[8,128]{1,0:T(8,128)}) custom-call(bf16[768,512]{1,0:T(8,128)(2,1)} %get-tuple-element.61.refs_0_, bf16[768,512]{1,0:T(8,128)(2,1)} %get-tuple-element.62.refs_1_, bf16[768,512]{1,0:T(8,128)(2,1)} %get-tuple-element.63.refs_2_, ...), custom_call_target="tpu_custom_call" | custom-call | tf_op jit(solution)/shard_map/reduce/pallas_call | solution.py:494
  222.2 3.2 %finish.1 = (f32[24,2304]{1,0:T(8,128)}, f32[24,768]{1,0:T(8,128)}, f32[24,3072]{1,0:T(8,128)}, f32[96,768]{1,0:T(8,128)}, f32[1,24]{1,0:T(1,128)}, /*index=5*/f...) custom-call(f32[8,128]{1,0:T(8,128)} %get-tuple-element.77.packed, ...), custom_call_target="tpu_custom_call" | custom-call | tf_op jit(solution)/shard_map/finish/pallas_call | solution.py:525
  (10 shorter events, 0.1 us)

commit v2 on v1

--- a/solution.py
+++ b/solution.py
@@ -558,7 +558,7 @@
     return scale * (grad - jnp.mean(grad, axis=-1, keepdims=True) - unit * jnp.mean(grad * unit, axis=-1, keepdims=True))
 
 
-def block_kernel(chunk, sections, key_ok, hidden, cotangent, g1, b1, qkv_b, out_b, g2, b2, fc_b, proj_b,
+def block_kernel(chunk, prepare, sections, lengths, token_mask, hidden, cotangent, g1, b1, qkv_b, out_b, g2, b2, fc_b, proj_b,
                  qkv_hbm, out_hbm, fc_hbm, proj_hbm,
                  hidden_out, grad_hidden, a_t, o_t, c_t, g_t, dqkv_st, do_st, du_st, dm_st,
                  dg1, db1, dqkv_b, dout_b, dg2, db2, dfc_b, dproj_b,
@@ -571,11 +571,12 @@
         ((qkv_hbm, qkv_w), (out_hbm, out_w), (fc_hbm, fc_w), (proj_hbm, proj_w)))]
     for c in loads:
         c.start()
+    prepare()
     for ref in (dg1, db1, dqkv_b, dout_b, dg2, db2, dfc_b, dproj_b):
         ref[...] = jnp.zeros_like(ref)
     query = lax.broadcasted_iota(jnp.int32, (rows, 2 * rows), 0)
     key = lax.rem(lax.broadcasted_iota(jnp.int32, (rows, 2 * rows), 1), rows)
-    ok = jnp.broadcast_to(key_ok[...], (rows, 2 * rows)) > 0.5
+    ok = (key < lengths[0]) & (jnp.broadcast_to(jnp.concatenate([token_mask[...]] * 2, axis=1), (rows, 2 * rows)) == 1)
     allow[...] = jnp.where((key < query) & ok | (key == query), 1.0, 0.0)
     state[...] = hidden[...].astype(jnp.float32)
     first = lax.broadcasted_iota(jnp.int32, (rows, pair), 1) < HEAD_DIM
@@ -706,26 +707,89 @@
     grad_hidden[...] = state[...]
 
 
-def run_block(sections, key_valid, hidden, cotangent, attention, mlp):
-    g1, b1, qkv_w, qv_b, out_w, out_b = attention
-    g2, b2, fc_w, fc_b, proj_w, proj_b = mlp
+VECTORS = ("g1", "b1", "qv_b", "out_b", "g2", "b2", "fc_b", "proj_b")
+
+
+class Spread:
+    def __init__(self, devices, w):
+        n = devices * w
+
+        def owner(shape):
+            return jnp.floor((lax.broadcasted_iota(jnp.int32, shape, 1).astype(jnp.float32) + 0.5) * (1.0 / w))
+
+        place = lax.broadcasted_iota(jnp.int32, (128, n), 1).astype(jnp.float32) - owner((128, n)) * w
+        lane = lax.broadcasted_iota(jnp.int32, (128, n), 0).astype(jnp.float32)
+        self.pick = jnp.where(place == lane, 1.0, 0.0).astype(jnp.bfloat16)
+        self.mine = owner((devices, n)) == lax.broadcasted_iota(jnp.int32, (devices, n), 0).astype(jnp.float32)
+
+    def join(self, rows):
+        return jnp.sum(jnp.where(self.mine, dot(rows.astype(jnp.bfloat16), self.pick), 0.0), axis=0, keepdims=True)
+
+    def split(self, joined):
+        values = jnp.where(self.mine, jnp.broadcast_to(joined, self.mine.shape), 0.0)
+        high = values.astype(jnp.bfloat16)
+        low = (values - high.astype(jnp.float32)).astype(jnp.bfloat16)
+        return dot(high, self.pick, NT) + dot(low, self.pick, NT)
+
+
+def packed_kernel(chunk, chunks, *refs):
+    ins, packed, weights, outs = refs[:5], refs[5], refs[6:10], refs[10:20]
+    packed_out, rest = refs[20], refs[21:]
+    scratch, vectors, grads = rest[:-16], rest[-16:-8], rest[-8:]
+    devices = packed.shape[0] // 8
+    width = ins[3].shape[1]
+
+    def prepare():
+        for w in sorted(set(chunks)):
+            spread = Spread(devices, w)
+            for i, c in enumerate(chunks):
+                if c != w:
+                    continue
+                row = spread.join(packed[pl.ds(i, devices, stride=8), :])
+                if VECTORS[i] == "qv_b":
+                    vectors[i][:, :width] = row[:, :width]
+                    vectors[i][:, width:2 * width] = jnp.zeros((1, width), jnp.float32)
+                    vectors[i][:, 2 * width:] = row[:, width:]
+                else:
+                    vectors[i][...] = row
+
+    block_kernel(chunk, prepare, *ins, *vectors, *weights, *outs, *grads, *scratch)
+    for w in sorted(set(chunks)):
+        spread = Spread(devices, w)
+        for i, c in enumerate(chunks):
+            if c == w:
+                row = grads[i][...]
+                if VECTORS[i] == "qv_b":
+                    row = jnp.concatenate([row[:, :width], row[:, 2 * width:]], axis=1)
+                packed_out[pl.ds(i, devices, stride=8), :] = spread.split(row)
+
+
+def run_block(sections, lengths, token_mask, hidden, cotangent, vectors, chunks, weights):
+    packed = chunks is not None
+    qkv_w, out_w, fc_w, proj_w = weights
     rows, width = hidden.shape
     ff = fc_w.shape[1]
-    bias = jnp.concatenate([qv_b[:width], jnp.zeros_like(qv_b[:width]), qv_b[width:]])
-    vectors = [v.astype(jnp.float32)[None] for v in (g1, b1, bias, out_b, g2, b2, fc_b, proj_b)]
-    key_ok = jnp.concatenate([key_valid, key_valid], axis=1).astype(jnp.float32)
     low, high = jnp.bfloat16, jnp.float32
+    sizes = [width, width, 3 * width, width, width, width, ff, width]
+    if packed:
+        given = [vectors]
+    else:
+        qv_b = vectors[2]
+        bias = jnp.concatenate([qv_b[:width], jnp.zeros_like(qv_b[:width]), qv_b[width:]])
+        given = [v.astype(high)[None] for v in (*vectors[:2], bias, *vectors[3:])]
     lefts, rights = [width, width, width, ff], [3 * width, width, ff, width]
     pairs = width // (2 * HEAD_DIM)
-    vmem, everywhere = pl.BlockSpec(memory_space=pltpu.VMEM), pl.BlockSpec(memory_space=pl.ANY)
+    chunk = 512 if ff % 512 == 0 and width * 3 % 512 == 0 else 256
+    smem, vmem, everywhere = [pl.BlockSpec(memory_space=m) for m in (pltpu.SMEM, pltpu.VMEM, pl.ANY)]
+    rows_of = [pltpu.VMEM((1, n), high) for n in sizes]
     outs = pl.pallas_call(
-        functools.partial(block_kernel, 512 if ff % 512 == 0 and width * 3 % 512 == 0 else 256),
+        functools.partial(packed_kernel, chunk, chunks) if packed else functools.partial(block_kernel, chunk, lambda: None),
         out_shape=[jax.ShapeDtypeStruct((rows, width), low), jax.ShapeDtypeStruct((rows, width), high)]
         + [jax.ShapeDtypeStruct((n, PASSES * rows), low) for n in lefts]
         + [jax.ShapeDtypeStruct((PASSES, rows, n), low) for n in rights]
-        + [jax.ShapeDtypeStruct(v.shape, high) for v in vectors],
-        in_specs=[pl.BlockSpec(memory_space=pltpu.SMEM)] + [vmem] * 11 + [everywhere] * 4,
-        out_specs=[vmem] * 18,
+        + [jax.ShapeDtypeStruct(v.shape, high) for v in given],
+        in_specs=[smem] * 2 + [vmem] * (3 + len(given)) + [everywhere] * 4,
+        out_specs=[vmem] * (10 + len(given)),
         scratch_shapes=[pltpu.VMEM(w.shape, low) for w in (qkv_w, out_w, fc_w, proj_w)] + [
             pltpu.VMEM((rows, width), high),
             pltpu.VMEM((PASSES, rows, width), high),
@@ -739,75 +803,40 @@
             pltpu.VMEM((rows, ff), low),
             pltpu.VMEM((rows, 2 * rows), high),
             pltpu.SemaphoreType.DMA((4,)),
-        ],
+        ] + (rows_of * 2 if packed else []),
         compiler_params=pltpu.CompilerParams(vmem_limit_bytes=67000000),
         name="block",
-    )(sections, key_ok, hidden, cotangent, *vectors, qkv_w, out_w, fc_w, proj_w)
+    )(sections, lengths, token_mask, hidden, cotangent, *given, qkv_w, out_w, fc_w, proj_w)
     hidden_out, grad_hidden = outs[:2]
     a, o, c, g = outs[2:6]
     dqkv, do, du, dm = [s.reshape(PASSES * rows, -1) for s in outs[6:10]]
-    dg1, db1, dbias, dout_b, dg2, db2, dfc_b, dproj_b = [v[0] for v in outs[10:]]
-    dqv_b = jnp.concatenate([dbias[:width], dbias[2 * width:]])
     factors = ((a, dqkv), (o, do), (c, du), (g, dm))
-    return hidden_out, grad_hidden, factors, (dg1, db1, dqv_b, dout_b, dg2, db2, dfc_b, dproj_b)
-
-
-def fetch_attention(ln1_gain, ln1_bias, qkv_weight, qv_bias, out_weight, out_bias):
-    return (
-        lax.all_gather(ln1_gain, ("dp", "fsdp"), axis=0, tiled=True),
-        lax.all_gather(ln1_bias, ("dp", "fsdp"), axis=0, tiled=True),
-        lax.all_gather(qkv_weight, ("dp", "fsdp"), axis=0, tiled=True),
-        lax.all_gather(qv_bias, ("dp", "fsdp"), axis=0, tiled=True),
-        lax.all_gather(out_weight, ("dp", "fsdp"), axis=0, tiled=True),
-        lax.all_gather(out_bias, ("dp", "fsdp"), axis=0, tiled=True),
-    )
-
-
-def fetch_mlp(ln2_gain, ln2_bias, fc_weight, fc_bias, proj_weight, proj_bias):
-    return (
-        lax.all_gather(ln2_gain, ("dp", "fsdp"), axis=0, tiled=True),
-        lax.all_gather(ln2_bias, ("dp", "fsdp"), axis=0, tiled=True),
-        lax.all_gather(fc_weight, ("dp", "fsdp"), axis=0, tiled=True),
-        lax.all_gather(fc_bias, ("dp", "fsdp"), axis=0, tiled=True),
-        lax.all_gather(proj_weight, ("dp", "fsdp"), axis=0, tiled=True),
-        lax.all_gather(proj_bias, ("dp", "fsdp"), axis=0, tiled=True),
-    )
-
-
-def fetch_all(sizes, attention, mlp):
-    ln1_gain, ln1_bias, qkv_weight, qv_bias, out_weight, out_bias = attention
-    ln2_gain, ln2_bias, fc_weight, fc_bias, proj_weight, proj_bias = mlp
-    big = (qkv_weight, out_weight, fc_weight, proj_weight)
-    small = (ln1_gain, ln1_bias, qv_bias, out_bias, ln2_gain, ln2_bias, fc_bias, proj_bias)
-    width = -(-sum(v.shape[0] for v in small) // 1024) * 128
+    if packed:
+        return hidden_out, grad_hidden, factors, outs[10]
+    grads = [v[0] for v in outs[10:]]
+    grads[2] = jnp.concatenate([grads[2][:width], grads[2][2 * width:]])
+    return hidden_out, grad_hidden, factors, grads
+
+
+def fetch_all(sizes, big, small):
     if any(w.shape[0] % 8 for w in big):
-        return fetch_attention(*attention), fetch_mlp(*mlp)
-    packed = jnp.concatenate(small)
-    packed = jnp.pad(packed, (0, 8 * width - packed.shape[0])).reshape(8, width)
-    *full, rows = gather(sizes, (*big, packed))
-    qkv_full, out_full, fc_full, proj_full = [w.reshape(-1, w.shape[-1]) for w in full]
-    rows = rows.reshape(-1, 8 * width)
-    vectors, start = [], 0
-    for v in small:
-        vectors.append(rows[:, start : start + v.shape[0]].reshape(-1))
-        start += v.shape[0]
-    g1, b1, qv, ob, g2, b2, fb, pb = vectors
-    return (g1, b1, qkv_full, qv, out_full, ob), (g2, b2, fc_full, fb, proj_full, pb)
-
-
-def sum_all(sizes, factors, vectors):
-    chips = sizes["x"] * sizes["y"] * sizes["z"]
-    if any(left.shape[0] % (16 * chips) for left, _ in factors):
+        whole = [lax.all_gather(v, ("dp", "fsdp"), axis=0, tiled=True) for v in (*big, *small)]
+        return whole[:4], whole[4:], None
+    chunks = tuple(v.shape[0] for v in small)
+    width = -(-max(chunks) // 128) * 128
+    packed = jnp.stack([jnp.pad(v.astype(jnp.float32), (0, width - v.shape[0])) for v in small])
+    *full, packed = [w.reshape(-1, w.shape[-1]) for w in gather(sizes, (*big, packed))]
+    return full, packed, chunks
+
+
+def sum_all(sizes, factors, vectors, chunks):
+    if chunks is None:
         big = [dot(left, right).astype(jnp.bfloat16) for left, right in factors]
         qkv, out, fc, proj, *sums = [
             lax.psum_scatter(v, ("dp", "fsdp"), scatter_dimension=0, tiled=True).astype(jnp.float32) for v in (*big, *vectors)
         ]
     else:
-        lead = (sizes["x"], 2, sizes["z"], sizes["y"])
-        chunks = [v.shape[0] // (2 * chips) for v in vectors]
-        width = -(-max(chunks) // 128) * 128
-        rows = [jnp.pad(v.reshape(2 * chips, 1, w), ((0, 0), (0, 0), (0, width - w))) for v, w in zip(vectors, chunks)]
-        packed = jnp.concatenate(rows, axis=1).reshape(*lead, 8, width)
+        packed = vectors.reshape(sizes["x"], 2, sizes["z"], sizes["y"], 8, -1)
         *big, packed = reduce_scatter(sizes, factors, packed)
         (qkv, out, fc, proj), sums = finish(chunks, big, packed)
     g1, b1, qv, ob, g2, b2, fb, pb = sums
@@ -836,19 +865,16 @@
 ):
     seq_count, seq_len, model_width = hidden.shape
     row_count = seq_count * seq_len
-    key_pos = jnp.arange(seq_len, dtype=jnp.int32)
-    key_valid = (key_pos[None, :] < lengths[:, None]) & (token_mask == 1)
-
-    current = fetch_all(
+    weights, vectors, chunks = fetch_all(
         sizes,
-        (ln1_gain, ln1_bias, qkv_weight, qv_bias, out_weight, out_bias),
-        (ln2_gain, ln2_bias, fc_weight, fc_bias, proj_weight, proj_bias),
+        (qkv_weight, out_weight, fc_weight, proj_weight),
+        (ln1_gain, ln1_bias, qv_bias, out_bias, ln2_gain, ln2_bias, fc_bias, proj_bias),
     )
-
-    hidden_out, grad_hidden, factors, vectors = run_block(
-        sections, key_valid, hidden.reshape(row_count, model_width), cotangent.reshape(row_count, model_width), *current
+    hidden_out, grad_hidden, factors, terms = run_block(
+        sections, lengths, token_mask, hidden.reshape(row_count, model_width), cotangent.reshape(row_count, model_width),
+        vectors, chunks, weights,
     )
-    attention_grads, finished = sum_all(sizes, factors, vectors)
+    attention_grads, finished = sum_all(sizes, factors, terms, chunks)
     hidden_out = hidden_out.reshape(hidden.shape)
     grad_hidden = grad_hidden.reshape(hidden.shape)
     return (

time: 226 us -> 207 us (0.916)
  local copies, waits for them, and re-layouts: 14.6 us -> 2.74 us
  other arithmetic: 7.56 us -> 0.6 us
    concatenate x8 -> x0, local copies, waits for them, and re-layouts: 6.5 us -> none  [the longest x1 5.43 us: fetch_all(): packed = jnp.concatenate(small)]
    pallas_call x7 -> x0, other arithmetic: 5.53 us -> none  [run_block(): pl.pallas_call(functools.partial(block_kernel, 512 if ff % 512 == 0 and w...]
    convert_element_type x7 -> x0, local copies, waits for them, and re-layouts: 4.76 us -> none  [run_block(): v.astype(jnp.float32)[None]]
where the time goes in v2:
time: 207 us
  Pallas kernels  201 us (97%)
  local copies, waits for them, and re-layouts  2.74 us (1%)
  between operations  2.14 us (1%)
    pallas_call x1, Pallas kernels, reduce_scatter(): pl.pallas_call(functools.partial(reduce_kernel, sizes, pieces, order, len...  83 us
    pallas_call x1, Pallas kernels, gather(): pl.pallas_call(functools.partial(gather_kernel, sizes, pieces, order, n_i...  63 us
    pallas_call x1, Pallas kernels, run_block(): pl.pallas_call(functools.partial(packed_kernel, chunk, chunks) if packed...  52.1 us

profile of v2, /device:TPU:0, one launch (start us, length us, event | category | flops | bytes accessed | tf_op | source)
XLA Modules:
  0.0 206.8 jit_solution(3783176643015641462)
XLA Ops:
  1.9 0.7 pad_bitcast_fusion.6
  2.6 0.7 pad_bitcast_fusion.4
  3.3 0.7 pad_bitcast_fusion.2
  4.0 0.7 pad_bitcast_fusion
  4.7 0.6 stack.46.refs_4_
  5.3 63.0 %gather.1 = (bf16[2,2,4,2,24,2304]{5,4,3,2,1,0:T(8,128)(2,1)}, bf16[2,2,4,2,24,768]{5,4,3,2,1,0:T(8,128)(2,1)}, bf16[2,2,4,2,24,3072]{5,4,3,2,1,0:T(8,128)(2,1)}...) custom-call(bf16[24,2304]{1,0:T(8,128)(2,1)} %refs_0_.2, bf16[24,768]{1,0:T(8,128)(2,1)} %refs_1_.2, ...), custom_call_target="tpu_custom_call" | custom-call | tf_op jit(solution)/shard_map/gather/pallas_call | solution.py:176
  68.2 52.1 %block.1 = (bf16[128,768]{1,0:T(8,128)(2,1)}, f32[128,768]{1,0:T(8,128)}, bf16[768,512]{1,0:T(8,128)(2,1)}, bf16[768,512]{1,0:T(8,128)(2,1)}, bf16[768,512]{1,0:...) custom-call(s32[1]{0:T(128)S(6)} %copy.31.refs_0_, ...), custom_call_target="tpu_custom_call" | custom-call | tf_op jit(solution)/shard_map/block/pallas_call | solution.py:785
  120.3 83.0 %reduce.1 = (f32[24,2304]{1,0:T(8,128)}, f32[24,768]{1,0:T(8,128)}, f32[24,3072]{1,0:T(8,128)}, f32[96,768]{1,0:T(8,128)}, f32[8,128]{1,0:T(8,128)}) custom-call(bf16[768,512]{1,0:T(8,128)(2,1)} %get-tuple-element.54.refs_0_, bf16[768,512]{1,0:T(8,128)(2,1)} %get-tuple-element.55.refs_1_, bf16[768,512]{1,0:T(8,128)(2,1)} %get-tuple-element.56.refs_2_, ...), custom_call_target="tpu_custom_call" | custom-call | tf_op jit(solution)/shard_map/reduce/pallas_call | solution.py:494
  203.3 3.2 %finish.1 = (f32[24,2304]{1,0:T(8,128)}, f32[24,768]{1,0:T(8,128)}, f32[24,3072]{1,0:T(8,128)}, f32[96,768]{1,0:T(8,128)}, f32[1,24]{1,0:T(1,128)}, /*index=5*/f...) custom-call(f32[8,128]{1,0:T(8,128)} %get-tuple-element.63.packed, ...), custom_call_target="tpu_custom_call" | custom-call | tf_op jit(solution)/shard_map/finish/pallas_call | solution.py:525
  (1 shorter events, 0.0 us)

commit v3 on v2

--- a/solution.py
+++ b/solution.py
@@ -78,7 +78,7 @@
 
     def part(pi, at, who):
         a, tree, lo, n = pieces[pi]
-        return outs[a].at[at["x"], who, at["z"], at["y"], pl.ds(lo, n)]
+        return outs[a].at[at["x"], who, at["z"], at["y"], :, pl.ds(lo, n)]
 
     def remote(src, dst, send, recv, dev):
         return pltpu.make_async_remote_copy(src_ref=src, dst_ref=dst, send_sem=send, recv_sem=recv, device_id=dev, device_id_type=MESH)
@@ -107,7 +107,7 @@
                 conds.append((at[d] >= 0) if v < 0 else (at[d] < sizes[d]))
         chip = place.chip(at)
         dst = part(pi, at, core)
-        src = ins[a].at[pl.ds(lo, n)] if own else dst
+        src = ins[a].at[:, pl.ds(lo, n)] if own else dst
         k = max([j for j, v in enumerate(t) if v != 0], default=-1)
 
         def handle(tree=tree, t=t, own=own, chip=chip, dst=dst, src=src, k=k, pi=pi):
@@ -162,15 +162,11 @@
     chips = sizes["x"] * sizes["y"] * sizes["z"]
     pieces = []
     for a, s in enumerate(shards):
-        tiles = s.shape[0] // 8
-        if tiles % 3 == 0 and tiles < 12:
-            cuts = [(i, i * tiles // 3, tiles // 3) for i in range(3)]
-        elif tiles % 2 == 0:
-            cuts = [(i, i * tiles // 2, tiles // 2) for i in range(2)]
-        else:
-            cuts = [(2, 0, tiles)]
-        for tree, lo, n in cuts:
-            pieces.append((a, TREES[tree], lo * 8, n * 8))
+        tiles = s.shape[1] // 128
+        first = [round(tiles * v) for v in ((0.0, 0.375, 0.78, 1.0) if a % 2 else (0.0, 0.4, 0.78, 1.0))]
+        for tree, lo, hi in zip(TREES, first, first[1:]):
+            if hi > lo:
+                pieces.append((a, tree, lo * 128, (hi - lo) * 128))
     order = gather_order(sizes, pieces, alpha)
     n_in = len(shards)
     return pl.pallas_call(

time: 207 us -> 210 us (1.014)
  Pallas kernels: 201 us -> 204 us
    pallas_call x1, Pallas kernels: 63 us -> 65.5 us  [gather(): pl.pallas_call(functools.partial(gather_kernel, sizes, pieces, order, n_i...]
where the time goes in v3:
time: 210 us; the launch traced here: 209 us
  Pallas kernels  204 us (97%)
  local copies, waits for them, and re-layouts  2.74 us (1%)
  between operations  2.16 us (1%)
    pallas_call x1, Pallas kernels, reduce_scatter(): pl.pallas_call(functools.partial(reduce_kernel, sizes, pieces, order, len...  83 us
    pallas_call x1, Pallas kernels, gather(): pl.pallas_call(functools.partial(gather_kernel, sizes, pieces, order, n_i...  65.5 us
    pallas_call x1, Pallas kernels, run_block(): pl.pallas_call(functools.partial(packed_kernel, chunk, chunks) if packed...  52.1 us

profile of v3, /device:TPU:0, one launch (start us, length us, event | category | flops | bytes accessed | tf_op | source)
XLA Modules:
  0.0 209.3 jit_solution(9307943912863898437)
XLA Ops:
  1.9 0.7 pad_bitcast_fusion.6
  2.6 0.7 pad_bitcast_fusion.4
  3.3 0.7 pad_bitcast_fusion.2
  4.0 0.7 pad_bitcast_fusion
  4.7 0.6 stack.46.refs_4_
  5.3 65.5 %gather.1 = (bf16[2,2,4,2,24,2304]{5,4,3,2,1,0:T(8,128)(2,1)}, bf16[2,2,4,2,24,768]{5,4,3,2,1,0:T(8,128)(2,1)}, bf16[2,2,4,2,24,3072]{5,4,3,2,1,0:T(8,128)(2,1)}...) custom-call(bf16[24,2304]{1,0:T(8,128)(2,1)} %refs_0_.2, bf16[24,768]{1,0:T(8,128)(2,1)} %refs_1_.2, ...), custom_call_target="tpu_custom_call" | custom-call | tf_op jit(solution)/shard_map/gather/pallas_call | solution.py:172
  70.8 52.1 %block.1 = (bf16[128,768]{1,0:T(8,128)(2,1)}, f32[128,768]{1,0:T(8,128)}, bf16[768,512]{1,0:T(8,128)(2,1)}, bf16[768,512]{1,0:T(8,128)(2,1)}, bf16[768,512]{1,0:...) custom-call(s32[1]{0:T(128)S(6)} %copy.31.refs_0_, ...), custom_call_target="tpu_custom_call" | custom-call | tf_op jit(solution)/shard_map/block/pallas_call | solution.py:781
  122.9 83.0 %reduce.1 = (f32[24,2304]{1,0:T(8,128)}, f32[24,768]{1,0:T(8,128)}, f32[24,3072]{1,0:T(8,128)}, f32[96,768]{1,0:T(8,128)}, f32[8,128]{1,0:T(8,128)}) custom-call(bf16[768,512]{1,0:T(8,128)(2,1)} %get-tuple-element.54.refs_0_, bf16[768,512]{1,0:T(8,128)(2,1)} %get-tuple-element.55.refs_1_, bf16[768,512]{1,0:T(8,128)(2,1)} %get-tuple-element.56.refs_2_, ...), custom_call_target="tpu_custom_call" | custom-call | tf_op jit(solution)/shard_map/reduce/pallas_call | solution.py:490
  205.9 3.2 %finish.1 = (f32[24,2304]{1,0:T(8,128)}, f32[24,768]{1,0:T(8,128)}, f32[24,3072]{1,0:T(8,128)}, f32[96,768]{1,0:T(8,128)}, f32[1,24]{1,0:T(1,128)}, /*index=5*/f...) custom-call(f32[8,128]{1,0:T(8,128)} %get-tuple-element.63.packed, ...), custom_call_target="tpu_custom_call" | custom-call | tf_op jit(solution)/shard_map/finish/pallas_call | solution.py:521
  (1 shorter events, 0.0 us)

commit v4 on v2

--- a/solution.py
+++ b/solution.py
@@ -824,7 +824,10 @@
         return whole[:4], whole[4:], None
     chunks = tuple(v.shape[0] for v in small)
     width = -(-max(chunks) // 128) * 128
-    packed = jnp.stack([jnp.pad(v.astype(jnp.float32), (0, width - v.shape[0])) for v in small])
+    count = len(small)
+    packed = sum(
+        jnp.pad(v.astype(jnp.float32)[None], ((i, count - 1 - i), (0, width - v.shape[0]))) for i, v in enumerate(small)
+    )
     *full, packed = [w.reshape(-1, w.shape[-1]) for w in gather(sizes, (*big, packed))]
     return full, packed, chunks
 

time: 207 us -> 205 us (level)
  local copies, waits for them, and re-layouts: 2.74 us -> 0 us
    another operation x5 -> x0, local copies, waits for them, and re-layouts: 2.74 us -> none  [fetch_all(): jnp.stack([jnp.pad(v.astype(jnp.float32), (0, width - v.shape[0])) for v...]
where the time goes in v4:
time: 205 us
  Pallas kernels  201 us (98%)
  between operations  2.15 us (1%)
    pallas_call x1, Pallas kernels, reduce_scatter(): pl.pallas_call(functools.partial(reduce_kernel, sizes, pieces, order, len...  83.1 us
    pallas_call x1, Pallas kernels, gather(): pl.pallas_call(functools.partial(gather_kernel, sizes, pieces, order, n_i...  63 us
    pallas_call x1, Pallas kernels, run_block(): pl.pallas_call(functools.partial(packed_kernel, chunk, chunks) if packed...  52 us

profile of v4, /device:TPU:0, one launch (start us, length us, event | category | flops | bytes accessed | tf_op | source)
XLA Modules:
  0.0 204.9 jit_solution(695095641290168436)
XLA Ops:
  1.9 1.4 convert_add_fusion.refs_4_
  3.3 63.0 %gather.1 = (bf16[2,2,4,2,24,2304]{5,4,3,2,1,0:T(8,128)(2,1)}, bf16[2,2,4,2,24,768]{5,4,3,2,1,0:T(8,128)(2,1)}, bf16[2,2,4,2,24,3072]{5,4,3,2,1,0:T(8,128)(2,1)}...) custom-call(bf16[24,2304]{1,0:T(8,128)(2,1)} %refs_0_.2, bf16[24,768]{1,0:T(8,128)(2,1)} %refs_1_.2, ...), custom_call_target="tpu_custom_call" | custom-call | tf_op jit(solution)/shard_map/gather/pallas_call | solution.py:176
  66.3 52.0 %block.1 = (bf16[128,768]{1,0:T(8,128)(2,1)}, f32[128,768]{1,0:T(8,128)}, bf16[768,512]{1,0:T(8,128)(2,1)}, bf16[768,512]{1,0:T(8,128)(2,1)}, bf16[768,512]{1,0:...) custom-call(s32[1]{0:T(128)S(6)} %copy.31.refs_0_, ...), custom_call_target="tpu_custom_call" | custom-call | tf_op jit(solution)/shard_map/block/pallas_call | solution.py:785
  118.3 83.1 %reduce.1 = (f32[24,2304]{1,0:T(8,128)}, f32[24,768]{1,0:T(8,128)}, f32[24,3072]{1,0:T(8,128)}, f32[96,768]{1,0:T(8,128)}, f32[8,128]{1,0:T(8,128)}) custom-call(bf16[768,512]{1,0:T(8,128)(2,1)} %get-tuple-element.54.refs_0_, bf16[768,512]{1,0:T(8,128)(2,1)} %get-tuple-element.55.refs_1_, bf16[768,512]{1,0:T(8,128)(2,1)} %get-tuple-element.56.refs_2_, ...), custom_call_target="tpu_custom_call" | custom-call | tf_op jit(solution)/shard_map/reduce/pallas_call | solution.py:494
  201.5 3.2 %finish.1 = (f32[24,2304]{1,0:T(8,128)}, f32[24,768]{1,0:T(8,128)}, f32[24,3072]{1,0:T(8,128)}, f32[96,768]{1,0:T(8,128)}, f32[1,24]{1,0:T(1,128)}, /*index=5*/f...) custom-call(f32[8,128]{1,0:T(8,128)} %get-tuple-element.63.packed, ...), custom_call_target="tpu_custom_call" | custom-call | tf_op jit(solution)/shard_map/finish/pallas_call | solution.py:525

commit v5 on v4

--- a/solution.py
+++ b/solution.py
@@ -504,17 +504,13 @@
 
 
 def finish_kernel(chunks, packed, *refs):
-    n = (len(refs) - 1 - len(chunks)) // 3
-    ins, outs, vectors, bufs, sems = refs[:n], refs[n:2 * n], refs[2 * n:2 * n + len(chunks)], refs[2 * n + len(chunks):-1], refs[-1]
-    loads = [pltpu.make_async_copy(a, b, sems.at[0, i]) for i, (a, b) in enumerate(zip(ins, bufs))]
-    stores = [pltpu.make_async_copy(b, o, sems.at[1, i]) for i, (b, o) in enumerate(zip(bufs, outs))]
-    for c in loads:
-        c.start()
+    n = (len(refs) - 1 - len(chunks)) // 2
+    ins, outs, vectors, sems = refs[:n], refs[n:2 * n], refs[2 * n:-1], refs[-1]
+    stores = [pltpu.make_async_copy(a, o, sems.at[i]) for i, (a, o) in enumerate(zip(ins, outs))]
+    for o in stores:
+        o.start()
     for i, w in enumerate(chunks):
         vectors[i][...] = packed[i:i + 1, :w]
-    for c, o in zip(loads, stores):
-        c.wait()
-        o.start()
     for o in stores:
         o.wait()
 
@@ -525,9 +521,9 @@
     out = pl.pallas_call(
         functools.partial(finish_kernel, chunks),
         out_shape=[jax.ShapeDtypeStruct(a.shape, a.dtype) for a in arrays] + [jax.ShapeDtypeStruct((1, w), packed.dtype) for w in chunks],
-        in_specs=[vmem] + [everywhere] * n,
+        in_specs=[vmem] * (n + 1),
         out_specs=[everywhere] * n + [vmem] * len(chunks),
-        scratch_shapes=[pltpu.VMEM(a.shape, a.dtype) for a in arrays] + [pltpu.SemaphoreType.DMA((2, n))],
+        scratch_shapes=[pltpu.SemaphoreType.DMA((n,))],
         name="finish",
     )(packed, *arrays)
     return out[:n], [v[0] for v in out[n:]]

time: 205 us -> 205 us (level)
  no operation moved by 1% of the time
where the time goes in v5:
time: 205 us; the launch traced here: 204 us
  Pallas kernels  201 us (98%)
  between operations  2.15 us (1%)
    pallas_call x1, Pallas kernels, reduce_scatter(): pl.pallas_call(functools.partial(reduce_kernel, sizes, pieces, order, len...  83 us
    pallas_call x1, Pallas kernels, gather(): pl.pallas_call(functools.partial(gather_kernel, sizes, pieces, order, n_i...  63 us
    pallas_call x1, Pallas kernels, run_block(): pl.pallas_call(functools.partial(packed_kernel, chunk, chunks) if packed...  52 us

profile of v5, /device:TPU:0, one launch (start us, length us, event | category | flops | bytes accessed | tf_op | source)
XLA Modules:
  0.0 204.3 jit_solution(982112456784632630)
XLA Ops:
  1.9 1.4 convert_add_fusion.refs_4_
  3.3 63.0 %gather.1 = (bf16[2,2,4,2,24,2304]{5,4,3,2,1,0:T(8,128)(2,1)}, bf16[2,2,4,2,24,768]{5,4,3,2,1,0:T(8,128)(2,1)}, bf16[2,2,4,2,24,3072]{5,4,3,2,1,0:T(8,128)(2,1)}...) custom-call(bf16[24,2304]{1,0:T(8,128)(2,1)} %refs_0_.2, bf16[24,768]{1,0:T(8,128)(2,1)} %refs_1_.2, ...), custom_call_target="tpu_custom_call" | custom-call | tf_op jit(solution)/shard_map/gather/pallas_call | solution.py:176
  66.3 52.0 %block.1 = (bf16[128,768]{1,0:T(8,128)(2,1)}, f32[128,768]{1,0:T(8,128)}, bf16[768,512]{1,0:T(8,128)(2,1)}, bf16[768,512]{1,0:T(8,128)(2,1)}, bf16[768,512]{1,0:...) custom-call(s32[1]{0:T(128)S(6)} %copy.31.refs_0_, ...), custom_call_target="tpu_custom_call" | custom-call | tf_op jit(solution)/shard_map/block/pallas_call | solution.py:781
  118.3 83.0 %reduce.1 = (f32[24,2304]{1,0:T(8,128)}, f32[24,768]{1,0:T(8,128)}, f32[24,3072]{1,0:T(8,128)}, f32[96,768]{1,0:T(8,128)}, f32[8,128]{1,0:T(8,128)}) custom-call(bf16[768,512]{1,0:T(8,128)(2,1)} %get-tuple-element.54.refs_0_, bf16[768,512]{1,0:T(8,128)(2,1)} %get-tuple-element.55.refs_1_, bf16[768,512]{1,0:T(8,128)(2,1)} %get-tuple-element.56.refs_2_, ...), custom_call_target="tpu_custom_call" | custom-call | tf_op jit(solution)/shard_map/reduce/pallas_call | solution.py:494
  201.4 2.7 %finish.1 = (f32[24,2304]{1,0:T(8,128)}, f32[24,768]{1,0:T(8,128)}, f32[24,3072]{1,0:T(8,128)}, f32[96,768]{1,0:T(8,128)}, f32[1,24]{1,0:T(1,128)}, /*index=5*/f...) custom-call(f32[8,128]{1,0:T(8,128)} %get-tuple-element.63.packed, ...), custom_call_target="tpu_custom_call" | custom-call | tf_op jit(solution)/shard_map/finish/pallas_call | solution.py:521
